TPU v7x, 128 devices: a whole 4x4x4 slice. The times are simulated.
128 devices in a mesh: loop: 64 (over y, x, z_lo, core), rep: 2 (over z_hi).
Axes of the slice: x: 4, y: 4, z: 4 (z_hi: 2, z_lo: 2; z = z_hi * 2 + z_lo), core: 2. Of those that a mesh axis runs over, the one named last changes fastest.
Arguments:
- embeddings: bfloat16 [4096, 32, 1024], P('loop'), as said below
- lengths: int32 [4096], P('loop'), may hold values from 4 to 32
- candidate_ids: int32 [4096], P('loop'), may hold values from 0 to 255
Outputs:
- pair_scores: float32 [4096, 704], P('loop')
- consensus: float32 [4096], P('loop')
Inputs may be any that keep to these rules, and one draw needn't show every extreme that they name: Token embeddings of each candidate step.
All inputs are finite; a program needn't handle non-finite values.
Results may differ from a plain program's by a relative error of at most 0.0043.
Values may be sent and summed in bfloat16 or wider, within the bound.
A program may use at most 384 MiB of HBM per device.

v0:
```python
import jax, jax.numpy as jnp
from jax import lax
from jax.experimental import pallas as pl
from jax.experimental.pallas import tpu as pltpu
from jax.sharding import PartitionSpec as P

TOK = 32
HALF = 32
D = 1024
ROWS = TOK * HALF
GROUP = 16
CHUNK = 256


def prep_kernel(len_ref, meta_ref, emb_ref, out_ref, tmp):
    h, q = pl.program_id(0), pl.program_id(1)
    pos = lax.broadcasted_iota(jnp.int32, (TOK, 1), 0)

    def one(s, carry):
        x = emb_ref[s].astype(jnp.float32)
        ms = jnp.sum(x * x, axis=1, keepdims=True) * (1.0 / D)
        y = x * (lax.rsqrt(ms + 1e-06) * (1.0 / 32.0))
        n = len_ref[h * HALF + q * GROUP + s]
        y = jnp.where(pos < n, y, y[0:1, :])
        for k in range(D // 128):
            tmp[pl.ds(pl.multiple_of(k * GROUP * TOK + s * TOK, TOK), TOK), :] = y[:, k * 128:(k + 1) * 128]
        return carry

    lax.fori_loop(0, GROUP, one, 0, unroll=2)
    for t in range(TOK):
        for k in range(D // 128):
            rows = tmp[pl.ds(k * GROUP * TOK + t, GROUP, stride=TOK), :]
            out_ref[pl.ds(pl.multiple_of(t * HALF + q * GROUP, GROUP), GROUP), k * 128:(k + 1) * 128] = rows.astype(jnp.bfloat16)

    @pl.when(q == 0)
    def _():
        out_ref[ROWS:ROWS + 16, :] = meta_ref[...]


def prep(emb, lengths, meta):
    return pl.pallas_call(
        prep_kernel,
        grid=(2, HALF // GROUP),
        in_specs=[
            pl.BlockSpec(memory_space=pltpu.SMEM),
            pl.BlockSpec((None, 16, D), lambda h, q: (h, 0, 0)),
            pl.BlockSpec((GROUP, TOK, D), lambda h, q: (h * (HALF // GROUP) + q, 0, 0)),
        ],
        out_specs=pl.BlockSpec((None, ROWS + 16, D), lambda h, q: (h, 0, 0)),
        out_shape=jax.ShapeDtypeStruct((2, ROWS + 16, D), jnp.bfloat16),
        scratch_shapes=[pltpu.VMEM((GROUP * TOK * D // 128, 128), jnp.float32)],
    )(lengths, meta, emb)


def make_meta(lengths, ids):
    l = jnp.tile(lengths.reshape(2, 1, HALF), (1, 1, TOK)).astype(jnp.bfloat16)
    i = jnp.tile(ids.reshape(2, 1, HALF), (1, 1, TOK)).astype(jnp.bfloat16)
    return jnp.concatenate([l, i, jnp.zeros((2, 14, D), jnp.bfloat16)], axis=1)


def rows_of(x):
    return jnp.broadcast_to(x.astype(jnp.float32).reshape(2, HALF, 1), (2, HALF, 128))


OFFSETS = ((4, 5, -2, -1, 1), (4, 3, -2, -3, 1), (-4, -3, -2, -5, 1), (-4, -5, -2, 5, -3))


def taken_offsets(role):
    found = []
    for k in range(5):
        for other in range(4):
            if (other + OFFSETS[other][k]) % 4 == role:
                found.append(-OFFSETS[other][k])
    return found


def score_chunk(own_ref, vis_ref, best_ref, row_best_ref, n, first):
    for h in range(2):
        s = lax.dot_general(own_ref[h, 0:ROWS, :], vis_ref[n * CHUNK:(n + 1) * CHUNK, :],
                            (((1,), (1,)), ((), ())), preferred_element_type=jnp.float32)
        row_best_ref[h, :, n * CHUNK:(n + 1) * CHUNK] = jnp.max(s.reshape(TOK, HALF, CHUNK), axis=0)
        cb = s[:, 0:128]
        for k in range(1, CHUNK // 128):
            cb = jnp.maximum(cb, s[:, k * 128:(k + 1) * 128])
        best_ref[h] = cb if first else jnp.maximum(best_ref[h], cb)


def finish_scores(len_ref, id_ref, vis_ref, best_ref, row_best_ref, x_ref, t_ref):
    lane = lax.broadcasted_iota(jnp.int32, (1, 128), 1)
    extra = vis_ref[ROWS:ROWS + 16, :].astype(jnp.float32)
    col_len = extra[0:1, :]
    for h in range(2):
        row_len = len_ref[h]
        total = jnp.zeros((HALF, 128), jnp.float32)
        for t in range(TOK):
            b = best_ref[h, t * HALF:(t + 1) * HALF, :]
            b = jnp.maximum(b, pltpu.roll(b, 64, 1))
            b = jnp.maximum(b, pltpu.roll(b, 32, 1))
            total = total + jnp.where(row_len > float(t), b, 0.0)
        precision = total / row_len
        rec = jnp.zeros((HALF, 128), jnp.float32)
        for k in range(ROWS // 128):
            u = (lane // HALF + 4 * k).astype(jnp.float32)
            rec = rec + jnp.where(u < col_len[:, k * 128:(k + 1) * 128], row_best_ref[h, :, k * 128:(k + 1) * 128], 0.0)
        rec = rec + pltpu.roll(rec, 64, 1)
        rec = rec + pltpu.roll(rec, 32, 1)
        recall = rec / col_len[:, 0:128]
        x_ref[h * HALF:(h + 1) * HALF, :] = 2.0 * precision * recall / jnp.maximum(precision + recall, 0.5)
    x_ref[64:72, :] = jnp.broadcast_to(extra[1:2, 0:128], (8, 128))
    both = jnp.concatenate([x_ref[0:64, :], id_ref[...]], axis=0)
    t_ref[...] = both.T[0:HALF, :]


def assemble(role, id_ref, x_refs, t_refs, table_ref, sum_ref):
    lane = lax.broadcasted_iota(jnp.int32, (64, 128), 1)
    row = lax.broadcasted_iota(jnp.int32, (64, 128), 0)
    low = lane < 64
    first = (lane % 64) < 32
    ids = id_ref[...]

    def own(k):
        vals = jnp.where(first, x_refs[0](k)[0:64, :], x_refs[1](k)[0:64, :])
        theirs = jnp.where(first[0:8], x_refs[0](k)[64:72, :], x_refs[1](k)[64:72, :])
        return vals, jnp.concatenate([theirs] * 8, axis=0)

    def taken(k, upper):
        both = jnp.concatenate([t_refs[0](k)[...], t_refs[1](k)[...]], axis=0)
        turned = pltpu.roll(both, 64, 1)
        return (turned, both) if upper else (both, turned)

    for mine in range(4):
        @pl.when(role == mine)
        def _(mine=mine):
            taken_at = taken_offsets(mine)
            total = jnp.zeros((64, 128), jnp.float32)
            for p in range(6):
                parts = []
                for upper in range(2):
                    d = 2 * p + upper - 5
                    if d > 5:
                        parts.append(parts[0])
                        continue
                    if d == 0:
                        vals, theirs = own(0)
                        same = (theirs == ids) & ((lane % 64) != row)
                    else:
                        if d in OFFSETS[mine]:
                            vals, theirs = own(1 + OFFSETS[mine].index(d))
                        else:
                            vals, theirs = taken(1 + taken_at.index(d), upper)
                        same = theirs == ids
                    inside = (lane >= 64) if upper else low
                    total = total + jnp.where(same & inside, vals, 0.0)
                    parts.append(vals)
                tile = jnp.where(low, parts[0], parts[1])
                width = 128 if p < 5 else 64
                table_ref[:, p * 128:p * 128 + width] = tile[:, 0:width]
            sums = jnp.sum(total, axis=1, keepdims=True)
            sum_ref[...] = jnp.broadcast_to(sums, (64, 128)).T[0:1, :]


def score_kernel(len_ref, id_ref, own_ref, vis_ref, x_ref, t_ref, best, row_best):
    for n in range(ROWS // CHUNK):
        score_chunk(own_ref, vis_ref, best, row_best, n, n == 0)
    finish_scores(len_ref, id_ref, vis_ref, best, row_best, x_ref, t_ref)


def score(own, vis, len_rows, id_rows):
    return pl.pallas_call(
        score_kernel,
        in_specs=[pl.BlockSpec(memory_space=pltpu.VMEM)] * 4,
        out_specs=[pl.BlockSpec(memory_space=pltpu.VMEM)] * 2,
        out_shape=[jax.ShapeDtypeStruct((72, 128), jnp.float32), jax.ShapeDtypeStruct((HALF, 128), jnp.float32)],
        scratch_shapes=[pltpu.VMEM((2, ROWS, 128), jnp.float32), pltpu.VMEM((2, HALF, ROWS), jnp.float32)],
        cost_estimate=pl.CostEstimate(flops=4 * ROWS * ROWS * D, bytes_accessed=6 << 20, transcendentals=0),
        compiler_params=pltpu.CompilerParams(vmem_limit_bytes=32 << 20),
    )(len_rows, id_rows, own, vis)


def place_kernel(role_ref, id_ref, x0, t0, x1, t1, table_ref, sum_ref):
    x_refs = [lambda k, x=x: x[k] for x in (x0, x1)]
    t_refs = [lambda k, t=t: t[k - 1] for t in (t0, t1)]
    assemble(role_ref[0], id_ref, x_refs, t_refs, table_ref, sum_ref)


def place(role, id_rows, x0, t0, x1, t1):
    return pl.pallas_call(
        place_kernel,
        in_specs=[pl.BlockSpec(memory_space=pltpu.SMEM)] + [pl.BlockSpec(memory_space=pltpu.VMEM)] * 5,
        out_specs=[pl.BlockSpec(memory_space=pltpu.VMEM)] * 2,
        out_shape=[jax.ShapeDtypeStruct((64, 704), jnp.float32), jax.ShapeDtypeStruct((1, 64), jnp.float32)],
    )(role, id_rows, x0, t0, x1, t1)


def move(value, k, back=False):
    n = lax.axis_size("loop")
    pairs = [((b + OFFSETS[b % 4][k]) % n, b) for b in range(n)]
    if back:
        pairs = [(b, a) for a, b in pairs]
    return lax.ppermute(value, "loop", pairs)


def shards(embeddings, lengths, candidate_ids):
    rep = lax.axis_index("rep")
    role = (lax.axis_index("loop") % 4).astype(jnp.int32).reshape(1)
    own = prep(embeddings, lengths, make_meta(lengths, candidate_ids))
    mine = lax.dynamic_index_in_dim(own, rep, 0, keepdims=False)
    len_rows, id_rows = rows_of(lengths), rows_of(candidate_ids).reshape(64, 128)
    visitors = [mine] + [move(mine, k) for k in (4, 0, 1, 2, 3)]
    xs, ts = {}, {}
    for k, vis in zip((0, 5, 1, 2, 3, 4), visitors):
        xs[k], t = score(own, vis, len_rows, id_rows)
        if k:
            ts[k] = move(t, k - 1, back=True)
    x = jnp.stack([xs[k] for k in range(6)])
    t = jnp.stack([ts[k] for k in range(1, 6)])
    ox, ot = lax.ppermute((x, t), "rep", [(0, 1), (1, 0)])
    zero = rep == 0
    pick = lambda a, b: (jnp.where(zero, a, b), jnp.where(zero, b, a))
    (x0, x1), (t0, t1) = pick(x, ox), pick(t, ot)
    table, sums = place(role, id_rows, x0, t0, x1, t1)
    return table, sums.reshape(64)


def solution(mesh):
    placed = (P("loop", None, None), P("loop"), P("loop"))
    return jax.shard_map(
        shards, mesh=mesh, in_specs=placed, out_specs=(P("loop", None), P("loop")), check_vma=False
    )
```

profile of v0, /device:TPU:0, one launch (start us, length us, event | category | flops | bytes accessed | tf_op | source)
XLA Modules:
  0.0 240.5 jit_solution(13542209244005401151)
XLA Ops:
  0.6 0.7 fusion.16
  1.4 0.7 fusion.15
  2.1 0.1 convert_element_type.48
  2.2 0.1 convert_element_type.51
  2.4 0.1 convert_element_type.50
  2.6 0.7 maximum_maximum_fusion.meta_ref
  3.3 13.4 %shard_map.50.own_ref = bf16[2,1040,1024]{2,1,0:T(8,128)(2,1)} custom-call(s32[64]{0:T(128)} %len_ref.1, bf16[2,16,1024]{2,1,0:T(8,128)(2,1)} %maximum_maximum_fusion.meta_ref, bf16[64,32,1024]{2,1,0:T(8,128)(2,1)} %emb_ref.1), custom_call_target="tpu_custom_call" | custom-call | tf_op jit(solution)/shard_map/pallas_call | solution.py:41
  16.7 1.8 dynamic-slice_bitcast_fusion.vis_ref
  18.5 5.4 %collective-permute-start = (bf16[1040,1024]{1,0:T(8,128)(2,1)S(1)}, bf16[1040,1024]{1,0:T(8,128)(2,1)}, u32[]{:S(2)}, u32[]{:S(2)}) collective-permute-start(bf16[1040,1024]{1,0:T(8,128)(2,1)S(1)} %dynamic-slice_bitcast_fusion.vis_ref), channel_id=1, source_target_pairs={{8,0},{10,2},{124,4},{126,6},{16,8},{18,10},{4,12},{6,14},{24,16},... | collective-permute-start | bytes 6389768 | tf_op jit(solution)/shard_map/ppermute | solution.py:200
  23.9 3.2 %collective-permute-start.3 = (bf16[1040,1024]{1,0:T(8,128)(2,1)S(1)}, bf16[1040,1024]{1,0:T(8,128)(2,1)}, u32[]{:S(2)}, u32[]{:S(2)}) collective-permute-start(bf16[1040,1024]{1,0:T(8,128)(2,1)S(1)} %dynamic-slice_bitcast_fusion.vis_ref), channel_id=1, source_target_pairs={{126,0},{124,2},{122,4},{16,6},{6,8},{4,10},{2,12},{24,14},{14,16}... | collective-permute-start | bytes 6389768 | tf_op jit(solution)/shard_map/ppermute | solution.py:200
  27.3 2.2 copy-done
  29.5 5.6 %shard_map.51 = (f32[72,128]{1,0:T(8,128)S(1)}, f32[32,128]{1,0:T(8,128)}) custom-call(f32[2,32,128]{2,1,0:T(8,128)S(1)} %broadcast_in_dim.17.len_ref, f32[64,128]{1,0:T(8,128)S(1)} %broadcast_in_dim.15.id_ref, bf16[2,1040,1024]{2,1,0:T(8,128)(2,1)S(1)} %copy-done, bf16[1040,1024]{1,0:T(8,128)(2,1)S(1)} %dynamic-slice_bitcast_fusion.vis_ref), custom_call_target="tpu_custom_call" | custom-call | flops 4294967296 | bytes 6291456 | tf_op jit(solution)/shard_map/pallas_call | solution.py:169
  35.1 35.5 %collective-permute-done = bf16[1040,1024]{1,0:T(8,128)(2,1)} collective-permute-done((bf16[1040,1024]{1,0:T(8,128)(2,1)S(1)}, bf16[1040,1024]{1,0:T(8,128)(2,1)}, u32[]{:S(2)}, u32[]{:S(2)}) %collective-permute-start) | collective-permute-done | bytes 2129952 | tf_op jit(solution)/shard_map/ppermute | solution.py:200
  70.6 6.6 %shard_map.57 = (f32[6,72,128]{2,1,0:T(8,128)S(1)}, f32[32,128]{1,0:T(8,128)S(1)}) fusion(f32[6,72,128]{2,1,0:T(8,128)S(1)} %bitcast_dynamic-update-slice_fusion.5, f32[2,32,128]{2,1,0:T(8,128)S(1)} %broadcast_in_dim.17.len_ref, f32[64,128]{1,0:T(8,128)S(1)} %broadcast_in_dim.15.id_ref, bf16[2,1040,1024]{2,1,0:T(8,128)(2,1)S(1)} %copy-done, ...), kind=kCustom, calls=%fused_computation.10 | custom fusion | bytes 6508544 | tf_op jit(solution)/shard_map/pallas_call | solution.py:169
  77.2 0.2 collective-permute-start.6
  77.4 60.5 %collective-permute-done.1 = bf16[1040,1024]{1,0:T(8,128)(2,1)} collective-permute-done((bf16[1040,1024]{1,0:T(8,128)(2,1)S(1)}, bf16[1040,1024]{1,0:T(8,128)(2,1)}, u32[]{:S(2)}, u32[]{:S(2)}) %collective-permute-start.1) | collective-permute-done | bytes 2129952 | tf_op jit(solution)/shard_map/ppermute | solution.py:200
  137.9 6.6 %shard_map.56 = (f32[6,72,128]{2,1,0:T(8,128)S(1)}, f32[32,128]{1,0:T(8,128)S(1)}) fusion(f32[6,72,128]{2,1,0:T(8,128)S(1)} %get-tuple-element.38, f32[2,32,128]{2,1,0:T(8,128)S(1)} %broadcast_in_dim.17.len_ref, f32[64,128]{1,0:T(8,128)S(1)} %broadcast_in_dim.15.id_ref, bf16[2,1040,1024]{2,1,0:T(8,128)(2,1)S(1)} %copy-done, ...), kind=kCustom, calls=%fused_computation.9 | custom fusion | bytes 6508544 | tf_op jit(solution)/shard_map/pallas_call | solution.py:169
  144.6 19.4 %collective-permute-done.2 = bf16[1040,1024]{1,0:T(8,128)(2,1)} collective-permute-done((bf16[1040,1024]{1,0:T(8,128)(2,1)S(1)}, bf16[1040,1024]{1,0:T(8,128)(2,1)}, u32[]{:S(2)}, u32[]{:S(2)}) %collective-permute-start.2) | collective-permute-done | bytes 2129952 | tf_op jit(solution)/shard_map/ppermute | solution.py:200
  163.9 6.6 %shard_map.55 = (f32[6,72,128]{2,1,0:T(8,128)S(1)}, f32[32,128]{1,0:T(8,128)S(1)}) fusion(f32[6,72,128]{2,1,0:T(8,128)S(1)} %get-tuple-element.42, f32[2,32,128]{2,1,0:T(8,128)S(1)} %broadcast_in_dim.17.len_ref, f32[64,128]{1,0:T(8,128)S(1)} %broadcast_in_dim.15.id_ref, bf16[2,1040,1024]{2,1,0:T(8,128)(2,1)S(1)} %copy-done, ...), kind=kCustom, calls=%fused_computation.8 | custom fusion | bytes 6508544 | tf_op jit(solution)/shard_map/pallas_call | solution.py:169
  170.6 37.1 %collective-permute-done.3 = bf16[1040,1024]{1,0:T(8,128)(2,1)} collective-permute-done((bf16[1040,1024]{1,0:T(8,128)(2,1)S(1)}, bf16[1040,1024]{1,0:T(8,128)(2,1)}, u32[]{:S(2)}, u32[]{:S(2)}) %collective-permute-start.3) | collective-permute-done | bytes 2129952 | tf_op jit(solution)/shard_map/ppermute | solution.py:200
  207.7 6.6 %shard_map.54 = (f32[6,72,128]{2,1,0:T(8,128)S(1)}, f32[32,128]{1,0:T(8,128)S(1)}) fusion(f32[6,72,128]{2,1,0:T(8,128)S(1)} %get-tuple-element.34, f32[2,32,128]{2,1,0:T(8,128)S(1)} %broadcast_in_dim.17.len_ref, f32[64,128]{1,0:T(8,128)S(1)} %broadcast_in_dim.15.id_ref, bf16[2,1040,1024]{2,1,0:T(8,128)(2,1)S(1)} %copy-done, ...), kind=kCustom, calls=%fused_computation.7 | custom fusion | bytes 6508544 | tf_op jit(solution)/shard_map/pallas_call | solution.py:169
  214.3 0.3 collective-permute-start.9
  214.6 6.6 %shard_map.53 = (f32[6,72,128]{2,1,0:T(8,128)S(1)}, f32[32,128]{1,0:T(8,128)S(1)}) fusion(f32[6,72,128]{2,1,0:T(8,128)S(1)} %get-tuple-element.30, f32[2,32,128]{2,1,0:T(8,128)S(1)} %broadcast_in_dim.17.len_ref, f32[64,128]{1,0:T(8,128)S(1)} %broadcast_in_dim.15.id_ref, bf16[2,1040,1024]{2,1,0:T(8,128)(2,1)S(1)} %copy-done, ...), kind=kCustom, calls=%fused_computation.6 | custom fusion | bytes 6508544 | tf_op jit(solution)/shard_map/pallas_call | solution.py:169
  221.2 0.8 collective-permute-start.10
  222.1 0.2 collective-permute-done.9
  222.2 2.1 collective-permute-done.10
  224.4 3.6 %collective-permute-start.11 = (f32[5,32,128]{2,1,0:T(8,128)S(1)}, f32[5,32,128]{2,1,0:T(8,128)S(1)}, u32[]{:S(2)}, u32[]{:S(2)}) collective-permute-start(f32[5,32,128]{2,1,0:T(8,128)S(1)} %constant_dynamic-update-slice_fusion), channel_id=1, source_target_pairs={{0,1},{1,0},{2,3},{3,2},{4,5},{5,4},{6,7},{7,6},{8,9},{9,8},{10,11... | collective-permute-start | bytes 245768 | tf_op jit(solution)/shard_map/ppermute | solution.py:217
  228.0 2.6 %collective-permute-done.11 = f32[5,32,128]{2,1,0:T(8,128)S(1)} collective-permute-done((f32[5,32,128]{2,1,0:T(8,128)S(1)}, f32[5,32,128]{2,1,0:T(8,128)S(1)}, u32[]{:S(2)}, u32[]{:S(2)}) %collective-permute-start.11) | collective-permute-done | bytes 81952 | tf_op jit(solution)/shard_map/ppermute | solution.py:217
  230.6 0.7 broadcast_select_fusion.2
  231.3 6.4 %collective-permute-done.5 = f32[6,72,128]{2,1,0:T(8,128)S(1)} collective-permute-done((f32[6,72,128]{2,1,0:T(8,128)S(1)}, f32[6,72,128]{2,1,0:T(8,128)S(1)}, u32[]{:S(2)}, u32[]{:S(2)}) %collective-permute-start.5) | collective-permute-done | bytes 221216 | tf_op jit(solution)/shard_map/ppermute | solution.py:217
  237.6 0.8 broadcast_select_fusion
  238.4 2.1 shard_map.52
  (27 shorter events, 0.6 us)
Async XLA Ops:
  18.5 52.1 %collective-permute-start = (bf16[1040,1024]{1,0:T(8,128)(2,1)S(1)}, bf16[1040,1024]{1,0:T(8,128)(2,1)}, u32[]{:S(2)}, u32[]{:S(2)}) collective-permute-start(bf16[1040,1024]{1,0:T(8,128)(2,1)S(1)} %dynamic-slice_bitcast_fusion.vis_ref), channel_id=1, source_target_pairs={{8,0},{10,2},{124,4},{126,6},{16,8},{18,10},{4,12},{6,14},{24,16},... | collective-permute-start | bytes 6389768 | tf_op jit(solution)/shard_map/ppermute | solution.py:200
  23.9 114.1 %collective-permute-start.1 = (bf16[1040,1024]{1,0:T(8,128)(2,1)S(1)}, bf16[1040,1024]{1,0:T(8,128)(2,1)}, u32[]{:S(2)}, u32[]{:S(2)}) collective-permute-start(bf16[1040,1024]{1,0:T(8,128)(2,1)S(1)} %dynamic-slice_bitcast_fusion.vis_ref), channel_id=1, source_target_pairs={{10,0},{8,2},{126,4},{124,6},{18,8},{16,10},{6,12},{4,14},{26,16},... | collective-permute-start | bytes 6389768 | tf_op jit(solution)/shard_map/ppermute | solution.py:200
  23.9 140.1 %collective-permute-start.2 = (bf16[1040,1024]{1,0:T(8,128)(2,1)S(1)}, bf16[1040,1024]{1,0:T(8,128)(2,1)}, u32[]{:S(2)}, u32[]{:S(2)}) collective-permute-start(bf16[1040,1024]{1,0:T(8,128)(2,1)S(1)} %dynamic-slice_bitcast_fusion.vis_ref), channel_id=1, source_target_pairs={{124,0},{126,2},{0,4},{2,6},{4,8},{6,10},{8,12},{10,14},{12,16},{1... | collective-permute-start | bytes 6389768 | tf_op jit(solution)/shard_map/ppermute | solution.py:200
  23.9 183.8 %collective-permute-start.3 = (bf16[1040,1024]{1,0:T(8,128)(2,1)S(1)}, bf16[1040,1024]{1,0:T(8,128)(2,1)}, u32[]{:S(2)}, u32[]{:S(2)}) collective-permute-start(bf16[1040,1024]{1,0:T(8,128)(2,1)S(1)} %dynamic-slice_bitcast_fusion.vis_ref), channel_id=1, source_target_pairs={{126,0},{124,2},{122,4},{16,6},{6,8},{4,10},{2,12},{24,14},{14,16}... | collective-permute-start | bytes 6389768 | tf_op jit(solution)/shard_map/ppermute | solution.py:200
  27.0 187.5 %collective-permute-start.4 = (bf16[1040,1024]{1,0:T(8,128)(2,1)S(1)}, bf16[1040,1024]{1,0:T(8,128)(2,1)}, u32[]{:S(2)}, u32[]{:S(2)}) collective-permute-start(bf16[1040,1024]{1,0:T(8,128)(2,1)S(1)} %dynamic-slice_bitcast_fusion.vis_ref), channel_id=1, source_target_pairs={{2,0},{4,2},{6,4},{0,6},{10,8},{12,10},{14,12},{8,14},{18,16},{20,... | collective-permute-start | bytes 6389768 | tf_op jit(solution)/shard_map/ppermute | solution.py:200
  27.2 187.4 %copy-start.1 = (f32[64,128]{1,0:T(8,128)}, f32[64,128]{1,0:T(8,128)S(1)}, u32[]{:S(2)}) copy-start(f32[64,128]{1,0:T(8,128)S(1)} %broadcast_in_dim.15.id_ref) | copy-start | bytes 98308
  27.3 2.2 copy-start
  77.2 144.8 %collective-permute-start.6 = (f32[32,128]{1,0:T(8,128)S(1)}, f32[32,128]{1,0:T(8,128)S(1)}, u32[]{:S(2)}, u32[]{:S(2)}) collective-permute-start(f32[32,128]{1,0:T(8,128)S(1)} %get-tuple-element.39), channel_id=1, source_target_pairs={{0,8},{2,10},{4,124},{6,126},{8,16},{10,18},{12,4},{14,6},{16,24},... | collective-permute-start | bytes 49160 | tf_op jit(solution)/shard_map/ppermute | solution.py:200
  144.5 77.5 %collective-permute-start.7 = (f32[32,128]{1,0:T(8,128)S(1)}, f32[32,128]{1,0:T(8,128)S(1)}, u32[]{:S(2)}, u32[]{:S(2)}) collective-permute-start(f32[32,128]{1,0:T(8,128)S(1)} %get-tuple-element.43), channel_id=1, source_target_pairs={{0,10},{2,8},{4,126},{6,124},{8,18},{10,16},{12,6},{14,4},{16,26},... | collective-permute-start | bytes 49160 | tf_op jit(solution)/shard_map/ppermute | solution.py:200
  170.5 51.5 %collective-permute-start.8 = (f32[32,128]{1,0:T(8,128)S(1)}, f32[32,128]{1,0:T(8,128)S(1)}, u32[]{:S(2)}, u32[]{:S(2)}) collective-permute-start(f32[32,128]{1,0:T(8,128)S(1)} %get-tuple-element.35), channel_id=1, source_target_pairs={{0,124},{2,126},{4,0},{6,2},{8,4},{10,6},{12,8},{14,10},{16,12},{1... | collective-permute-start | bytes 49160 | tf_op jit(solution)/shard_map/ppermute | solution.py:200
  214.3 7.9 %collective-permute-start.9 = (f32[32,128]{1,0:T(8,128)S(1)}, f32[32,128]{1,0:T(8,128)S(1)}, u32[]{:S(2)}, u32[]{:S(2)}) collective-permute-start(f32[32,128]{1,0:T(8,128)S(1)} %get-tuple-element.31), channel_id=1, source_target_pairs={{0,126},{2,124},{4,122},{6,16},{8,6},{10,4},{12,2},{14,24},{16,14}... | collective-permute-start | bytes 49160 | tf_op jit(solution)/shard_map/ppermute | solution.py:200
  221.2 3.2 %collective-permute-start.10 = (f32[32,128]{1,0:T(8,128)S(1)}, f32[32,128]{1,0:T(8,128)S(1)}, u32[]{:S(2)}, u32[]{:S(2)}) collective-permute-start(f32[32,128]{1,0:T(8,128)S(1)} %get-tuple-element.47), channel_id=1, source_target_pairs={{0,2},{2,4},{4,6},{6,0},{8,10},{10,12},{12,14},{14,8},{16,18},{18,... | collective-permute-start | bytes 49160 | tf_op jit(solution)/shard_map/ppermute | solution.py:200
  224.4 6.2 %collective-permute-start.11 = (f32[5,32,128]{2,1,0:T(8,128)S(1)}, f32[5,32,128]{2,1,0:T(8,128)S(1)}, u32[]{:S(2)}, u32[]{:S(2)}) collective-permute-start(f32[5,32,128]{2,1,0:T(8,128)S(1)} %constant_dynamic-update-slice_fusion), channel_id=1, source_target_pairs={{0,1},{1,0},{2,3},{3,2},{4,5},{5,4},{6,7},{7,6},{8,9},{9,8},{10,11... | collective-permute-start | bytes 245768 | tf_op jit(solution)/shard_map/ppermute | solution.py:217
  228.0 9.7 %collective-permute-start.5 = (f32[6,72,128]{2,1,0:T(8,128)S(1)}, f32[6,72,128]{2,1,0:T(8,128)S(1)}, u32[]{:S(2)}, u32[]{:S(2)}) collective-permute-start(f32[6,72,128]{2,1,0:T(8,128)S(1)} %get-tuple-element.46), channel_id=1, source_target_pairs={{0,1},{1,0},{2,3},{3,2},{4,5},{5,4},{6,7},{7,6},{8,9},{9,8},{10,11... | collective-permute-start | bytes 663560 | tf_op jit(solution)/shard_map/ppermute | solution.py:217
where the time goes:
time: 242 us; the launch traced here: 241 us
  waiting for transfers between devices  164 us (68%)
  local copies, waits for them, and re-layouts  37.6 us (16%)
  Pallas kernels  21.1 us (9%)
  starting transfers between devices  13.6 us (6%)
  other arithmetic  3.66 us (2%)
    ppermute x10, waiting for transfers between devices, move(): return lax.ppermute(value, 'loop', pairs)  155 us
    pallas_call x5, local copies, waits for them, and re-layouts, score(): pl.pallas_call(score_kernel, in_specs=[pl.BlockSpec(memory_space=pltpu.VM...  32.9 us
    pallas_call x1, Pallas kernels, prep(): pl.pallas_call(prep_kernel, grid=(2, HALF // GROUP), in_specs=[pl.BlockSp...  13.4 us
    ppermute x10, starting transfers between devices, move(): return lax.ppermute(value, 'loop', pairs)  9.98 us
    ppermute x2, waiting for transfers between devices, shards(): ox, ot = lax.ppermute((x, t), 'rep', [(0, 1), (1, 0)])  8.95 us
    pallas_call x1, Pallas kernels, score(): pl.pallas_call(score_kernel, in_specs=[pl.BlockSpec(memory_space=pltpu.VM...  5.6 us
  transfers between devices with their start and end apart: 12, of which 8 were waited for; matrix products, arithmetic and copies ran while one was open for 14% of the time, Pallas kernels for 2%

commit v1 on v0

v1 whole, which is shorter than its diff:
```python
import jax, jax.numpy as jnp
from jax import lax
from jax.experimental import pallas as pl
from jax.experimental.pallas import tpu as pltpu
from jax.sharding import PartitionSpec as P

TOK = 32
HALF = 32
D = 1024
ROWS = TOK * HALF
GROUP = 16
CHUNK = 256
CHUNKS = ROWS // CHUNK
MESH = pl.DeviceIdType.MESH


def prep_kernel(len_ref, emb_ref, out_ref, tmp):
    h, q = pl.program_id(0), pl.program_id(1)
    pos = lax.broadcasted_iota(jnp.int32, (TOK, 1), 0)

    def one(s, carry):
        x = emb_ref[s].astype(jnp.float32)
        ms = jnp.sum(x * x, axis=1, keepdims=True) * (1.0 / D)
        y = x * (lax.rsqrt(ms + 1e-06) * (1.0 / 32.0))
        n = len_ref[h * HALF + q * GROUP + s]
        y = jnp.where(pos < n, y, y[0:1, :])
        for k in range(D // 128):
            tmp[pl.ds(pl.multiple_of(k * GROUP * TOK + s * TOK, TOK), TOK), :] = y[:, k * 128:(k + 1) * 128]
        return carry

    lax.fori_loop(0, GROUP, one, 0, unroll=2)
    for t in range(TOK):
        for k in range(D // 128):
            rows = tmp[pl.ds(k * GROUP * TOK + t, GROUP, stride=TOK), :]
            out_ref[t // 8, pl.ds(pl.multiple_of(t % 8 * HALF + q * GROUP, GROUP), GROUP), k * 128:(k + 1) * 128] = rows.astype(jnp.bfloat16)


def prep(emb, lengths):
    return pl.pallas_call(
        prep_kernel,
        grid=(2, HALF // GROUP),
        in_specs=[
            pl.BlockSpec(memory_space=pltpu.SMEM),
            pl.BlockSpec((GROUP, TOK, D), lambda h, q: (h * (HALF // GROUP) + q, 0, 0)),
        ],
        out_specs=pl.BlockSpec((None, CHUNKS, CHUNK, D), lambda h, q: (h, 0, 0, 0)),
        out_shape=jax.ShapeDtypeStruct((2, CHUNKS, CHUNK, D), jnp.bfloat16),
        scratch_shapes=[pltpu.VMEM((GROUP * TOK * D // 128, 128), jnp.float32)],
    )(lengths, emb)


def make_meta(lengths, ids):
    both = jnp.stack([lengths, ids]).astype(jnp.float32).reshape(2, 2, 1, HALF)
    both = jnp.tile(jnp.swapaxes(both, 0, 1), (1, 1, 4, 4)).reshape(2, 8, 128)
    return both


def rows_of(x):
    return jnp.broadcast_to(x.astype(jnp.float32).reshape(2, HALF, 1), (2, HALF, 128))


BLOCK_REACH = 5
OFFSETS = ((4, 5, -2, -1, 1), (4, 3, -2, -3, 1), (-4, -3, -2, -5, 1), (-4, -5, -2, 5, -3))


def taken_offsets(role):
    found = []
    for k in range(5):
        for other in range(4):
            if (other + OFFSETS[other][k]) % 4 == role:
                found.append(-OFFSETS[other][k])
    return found


def score_chunk(own_ref, cols, best_ref, row_best_ref, slot, n):
    for h in range(2):
        s = lax.dot_general(own_ref[h].reshape(ROWS, D), cols,
                            (((1,), (1,)), ((), ())), preferred_element_type=jnp.float32)
        row_best_ref[slot, h, n] = jnp.max(s.reshape(TOK, HALF, CHUNK), axis=0)
        cb = s[:, 0:128]
        for k in range(1, CHUNK // 128):
            cb = jnp.maximum(cb, s[:, k * 128:(k + 1) * 128])
        best_ref[slot, h] = jnp.maximum(best_ref[slot, h], cb)


def finish_scores(len_ref, id_ref, meta, best_ref, row_best_ref, slot, x_ref):
    lane = lax.broadcasted_iota(jnp.int32, (1, 128), 1)
    col_len = meta[0:1, :]
    for h in range(2):
        row_len = len_ref[h]
        total = jnp.zeros((HALF, 128), jnp.float32)
        for t in range(TOK):
            b = best_ref[slot, h, t * HALF:(t + 1) * HALF, :]
            b = jnp.maximum(b, pltpu.roll(b, 64, 1))
            b = jnp.maximum(b, pltpu.roll(b, 32, 1))
            total = total + jnp.where(row_len > float(t), b, 0.0)
        precision = total / row_len
        rec = jnp.zeros((HALF, 128), jnp.float32)
        for n in range(CHUNKS):
            for k in range(CHUNK // 128):
                u = (lane // HALF + 4 * (n * (CHUNK // 128) + k)).astype(jnp.float32)
                rec = rec + jnp.where(u < col_len, row_best_ref[slot, h, n, :, k * 128:(k + 1) * 128], 0.0)
        rec = rec + pltpu.roll(rec, 64, 1)
        rec = rec + pltpu.roll(rec, 32, 1)
        recall = rec / col_len
        x_ref[slot, h * HALF:(h + 1) * HALF, :] = 2.0 * precision * recall / jnp.maximum(precision + recall, 0.5)
    x_ref[slot, 64:72, :] = jnp.broadcast_to(meta[4:5, :], (8, 128))


def turn(x_ref, id_ref, slot, t_ref):
    both = jnp.concatenate([x_ref[slot, 0:64, :], id_ref[...]], axis=0)
    t_ref[slot] = both.T[0:HALF, :]


def main_kernel(len_ref, id_ref, meta_ref, own_ref, table_ref, sum_ref,
                vis, metas, best, row_best, x_mine, x_other, t_mine, t_got,
                send_sem, recv_sem, meta_send, meta_recv, x_send, x_recv, t_send, t_recv):
    n_loop = lax.axis_size("loop")
    b, r = lax.axis_index("loop"), lax.axis_index("rep")
    other = 1 - r
    role = b % 4
    is_a = role < 2
    early = 5 - 2 * (role // 2)
    late = 8 - early
    partner = b + 1 - 2 * (b % 2)

    def block(d):
        return (b + n_loop + d) % n_loop

    def copy(src, dst, ssem, rsem, blk, rp):
        return pltpu.make_async_remote_copy(src_ref=src, dst_ref=dst, send_sem=ssem, recv_sem=rsem,
                                            device_id={"loop": blk, "rep": rp}, device_id_type=MESH)

    barrier = pltpu.get_barrier_semaphore()
    peers = [(block(d), rp) for d in range(-BLOCK_REACH, BLOCK_REACH + 1) if d for rp in (r, other)]
    peers += [(b, other), (block(7), r), (block(-7), r)]
    for blk, rp in peers:
        pl.semaphore_signal(barrier, inc=1, device_id={"loop": blk, "rep": rp}, device_id_type=MESH)
    best[...] = jnp.full(best.shape, -4.0, jnp.float32)
    pl.semaphore_wait(barrier, len(peers))

    def move(kind, n, src, slot, blk, rp):
        return copy(src, vis.at[slot, n], send_sem.at[kind, n], recv_sem.at[slot, n], blk, rp)

    def arrived(slot, n):
        copy(vis.at[slot, n], vis.at[slot, n], send_sem.at[0, n], recv_sem.at[slot, n], partner, r).wait_recv()

    mine = own_ref.at[r]
    cross = own_ref.at[other]
    starts = {
        0: [(0, mine, 1, block(-4), r), (2, mine, 3, block(2), r)],
        1: [(4, mine, 5, block(-1), r), (0, mine, 1, block(-4), r), (5, mine, 0, block(4), r), (2, cross, 3, block(2), other)],
        2: [(0, mine, 1, block(4), r), (4, cross, 5, block(-1), other)],
        3: [(4, mine, 5, block(-1), r), (0, mine, 1, block(4), r)],
    }
    for me in range(4):
        @pl.when(role == me)
        def _(me=me):
            for n in range(CHUNKS):
                for kind, src, slot, blk, rp in starts[me]:
                    move(kind, n, src.at[n], slot, blk, rp).start()
            for k in range(5):
                d = taken_offsets(me)[k]
                copy(meta_ref.at[r], metas.at[k], meta_send.at[k], meta_recv.at[k], block(d), r).start()

    def after_early(n):
        return [(2, 7, vis.at[3, n], 5, block(1), r), (2, 3, vis.at[3, n], 4, block(-7), r)]

    def after_first(n):
        return [(0, 1, vis.at[1, n], 2, partner, r), (1, 1, vis.at[1, n], 2, partner, r),
                (2, 1, vis.at[1, n], 2, partner, r), (3, 1, vis.at[1, n], 2, partner, r),
                (2, 2, vis.at[1, n], 3, block(-2), r), (3, 2, vis.at[1, n], 3, block(-2), r)]

    def after_relay(n):
        return [(1, 6, vis.at[0, n], 4, block(1), r)]

    def after_late(n):
        return [(0, 3, vis.at[3, n], 4, partner, r), (1, 3, vis.at[3, n], 4, partner, r)]

    def forward(list_of, n):
        for me in range(4):
            todo = [x for x in list_of(n) if x[0] == me]
            if todo:
                @pl.when(role == me)
                def _(todo=todo):
                    for _, kind, src, slot, blk, rp in todo:
                        move(kind, n, src, slot, blk, rp).start()

    def compute(slot, n):
        score_chunk(own_ref, vis[slot, n], best, row_best, slot, n)

    def second_part(n):
        arrived(late, n)
        forward(after_late, n)
        compute(late, n)
        arrived(4, n)
        compute(4, n)

    def self_step(n, carry):
        score_chunk(own_ref, own_ref[r, n], best, row_best, 0, n)
        return carry

    lax.fori_loop(0, CHUNKS, self_step, 0)

    def step(n, carry):
        arrived(early, n)
        forward(after_early, n)
        compute(early, n)
        arrived(1, n)
        forward(after_first, n)
        compute(1, n)

        @pl.when(role == 1)
        def _():
            arrived(0, n)
            forward(after_relay, n)

        arrived(2, n)
        compute(2, n)

        @pl.when(n > 0)
        def _():
            second_part(n - 1)
        return carry

    lax.fori_loop(0, CHUNKS, step, 0)

    for k in range(5):
        copy(metas.at[k], metas.at[k], meta_send.at[k], meta_recv.at[k], partner, r).wait_recv()

    def results(slot, me):
        blk = block(OFFSETS[me][slot - 1])
        out = [copy(x_mine.at[slot], x_other.at[slot], x_send.at[slot], x_recv.at[slot], b, other)]
        for i, rp in enumerate((r, other)):
            out.append(copy(t_mine.at[slot], t_got.at[r, slot], t_send.at[i, slot], t_recv.at[r, slot], blk, rp))
        return out

    def finish(slot, meta):
        finish_scores(len_ref, id_ref, meta, best, row_best, slot, x_mine)

    finish(0, meta_ref[r])
    for slot in (early, 1, 2):
        finish(slot, metas[slot - 1])
        turn(x_mine, id_ref, slot, t_mine)
    second_part(CHUNKS - 1)
    own_result = copy(x_mine.at[0], x_other.at[0], x_send.at[0], x_recv.at[0], b, other)
    own_result.start()
    for me in range(4):
        @pl.when(role == me)
        def _(me=me):
            for slot in (5 if me < 2 else 3, 1, 2):
                for c in results(slot, me):
                    c.start()
    for slot in (late, 4):
        finish(slot, metas[slot - 1])
        turn(x_mine, id_ref, slot, t_mine)
    for me in range(4):
        @pl.when(role == me)
        def _(me=me):
            for slot in (3 if me < 2 else 5, 4):
                for c in results(slot, me):
                    c.start()
    for slot in range(6):
        copy(x_mine.at[slot], x_other.at[slot], x_send.at[slot], x_recv.at[slot], b, other).wait_recv()
    for slot in range(1, 6):
        for i in range(2):
            copy(t_mine.at[slot], t_got.at[i, slot], t_send.at[i, slot], t_recv.at[i, slot], b, other).wait_recv()

    xs = [lambda k: _Pick(r == 0, x_mine.at[k], x_other.at[k]), lambda k: _Pick(r == 0, x_other.at[k], x_mine.at[k])]
    ts = [lambda k: t_got.at[0, k], lambda k: t_got.at[1, k]]
    assemble(role, id_ref, xs, ts, table_ref, sum_ref)

    own_result.wait_send()
    for me in range(4):
        @pl.when(role == me)
        def _(me=me):
            for n in range(CHUNKS):
                for kind, src, slot, blk, rp in starts[me]:
                    move(kind, n, src.at[n], slot, blk, rp).wait_send()
                for list_of in (after_early, after_first, after_relay, after_late):
                    for who, kind, src, slot, blk, rp in list_of(n):
                        if who == me:
                            move(kind, n, src, slot, blk, rp).wait_send()
            for k in range(5):
                d = taken_offsets(me)[k]
                copy(meta_ref.at[r], metas.at[k], meta_send.at[k], meta_recv.at[k], block(d), r).wait_send()
            for slot in range(1, 6):
                for c in results(slot, me):
                    c.wait_send()


class _Pick:
    def __init__(self, take, one, two):
        self.take, self.one, self.two = take, one, two

    def __getitem__(self, at):
        return jnp.where(self.take, self.one[at], self.two[at])


def assemble(role, id_ref, x_refs, t_refs, table_ref, sum_ref):
    lane = lax.broadcasted_iota(jnp.int32, (64, 128), 1)
    row = lax.broadcasted_iota(jnp.int32, (64, 128), 0)
    low = lane < 64
    first = (lane % 64) < 32
    ids = id_ref[...]

    def own(k):
        vals = jnp.where(first, x_refs[0](k)[0:64, :], x_refs[1](k)[0:64, :])
        theirs = jnp.where(first[0:8], x_refs[0](k)[64:72, :], x_refs[1](k)[64:72, :])
        return vals, jnp.concatenate([theirs] * 8, axis=0)

    def taken(k, upper):
        both = jnp.concatenate([t_refs[0](k)[...], t_refs[1](k)[...]], axis=0)
        turned = pltpu.roll(both, 64, 1)
        return (turned, both) if upper else (both, turned)

    for mine in range(4):
        @pl.when(role == mine)
        def _(mine=mine):
            taken_at = taken_offsets(mine)
            total = jnp.zeros((64, 128), jnp.float32)
            for p in range(6):
                parts = []
                for upper in range(2):
                    d = 2 * p + upper - 5
                    if d > 5:
                        parts.append(parts[0])
                        continue
                    if d == 0:
                        vals, theirs = own(0)
                        same = (theirs == ids) & ((lane % 64) != row)
                    else:
                        if d in OFFSETS[mine]:
                            vals, theirs = own(1 + OFFSETS[mine].index(d))
                        else:
                            vals, theirs = taken(1 + taken_at.index(d), upper)
                        same = theirs == ids
                    inside = (lane >= 64) if upper else low
                    total = total + jnp.where(same & inside, vals, 0.0)
                    parts.append(vals)
                tile = jnp.where(low, parts[0], parts[1])
                width = 128 if p < 5 else 64
                table_ref[:, p * 128:p * 128 + width] = tile[:, 0:width]
            sums = jnp.sum(total, axis=1, keepdims=True)
            sum_ref[...] = jnp.broadcast_to(sums, (64, 128)).T[0:1, :]


def shards(embeddings, lengths, candidate_ids):
    own = prep(embeddings, lengths)
    vmem, dma = pltpu.VMEM, pltpu.SemaphoreType.DMA
    f32 = jnp.float32
    table, sums = pl.pallas_call(
        main_kernel,
        in_specs=[pl.BlockSpec(memory_space=pltpu.VMEM)] * 4,
        out_specs=[pl.BlockSpec(memory_space=pltpu.VMEM)] * 2,
        out_shape=[jax.ShapeDtypeStruct((64, 704), f32), jax.ShapeDtypeStruct((1, 64), f32)],
        scratch_shapes=[
            vmem((6, CHUNKS, CHUNK, D), jnp.bfloat16),
            vmem((5, 8, 128), f32),
            vmem((6, 2, ROWS, 128), f32),
            vmem((6, 2, CHUNKS, HALF, CHUNK), f32),
            vmem((6, 72, 128), f32),
            vmem((6, 72, 128), f32),
            vmem((6, HALF, 128), f32),
            vmem((2, 6, HALF, 128), f32),
            dma((8, CHUNKS)),
            dma((6, CHUNKS)),
            dma((5,)),
            dma((5,)),
            dma((6,)),
            dma((6,)),
            dma((2, 6)),
            dma((2, 6)),
        ],
        compiler_params=pltpu.CompilerParams(collective_id=0, has_side_effects=True, vmem_limit_bytes=56 << 20),
    )(rows_of(lengths), rows_of(candidate_ids).reshape(64, 128), make_meta(lengths, candidate_ids), own)
    return table, sums.reshape(64)


def solution(mesh):
    placed = (P("loop", None, None), P("loop"), P("loop"))
    return jax.shard_map(
        shards, mesh=mesh, in_specs=placed, out_specs=(P("loop", None), P("loop")), check_vma=False
    )
```

time: 242 us -> 137 us (0.57)
  waiting for transfers between devices: 164 us -> 0 us
  Pallas kernels: 21.1 us -> 128 us
  local copies, waits for them, and re-layouts: 37.6 us -> 6.35 us
  starting transfers between devices: 13.6 us -> 0 us
    ppermute x12 -> x0, waiting for transfers between devices: 164 us -> none  [the longest x10 155 us: move(): return lax.ppermute(value, 'loop', pairs)]
    pallas_call x2 -> x1, Pallas kernels: 7.68 us -> 115 us  [shards(): pl.pallas_call(main_kernel, in_specs=[pl.BlockSpec(memory_space=pltpu.VME...]
    pallas_call x5 -> x0, local copies, waits for them, and re-layouts: 32.9 us -> none  [score(): pl.pallas_call(score_kernel, in_specs=[pl.BlockSpec(memory_space=pltpu.VM...]
    ppermute x12 -> x0, starting transfers between devices: 13.6 us -> none  [the longest x10 9.98 us: move(): return lax.ppermute(value, 'loop', pairs)]
  transfers between devices with their start and end apart: 12 -> 0, of which waited for: 8 -> 0; matrix products, arithmetic and copies ran while one was open for 14% -> 0% of each run, Pallas kernels for 2% -> 0%
where the time goes in v1:
time: 137 us; the launch traced here: 136 us
  Pallas kernels  128 us (93%)
  local copies, waits for them, and re-layouts  6.35 us (5%)
    pallas_call x1, Pallas kernels, shards(): pl.pallas_call(main_kernel, in_specs=[pl.BlockSpec(memory_space=pltpu.VME...  115 us
    pallas_call x1, Pallas kernels, prep(): pl.pallas_call(prep_kernel, grid=(2, HALF // GROUP), in_specs=[pl.BlockSp...  13.4 us

profile of v1, /device:TPU:0, one launch (start us, length us, event | category | flops | bytes accessed | tf_op | source)
XLA Modules:
  0.0 136.3 jit_solution(945481661218559174)
XLA Ops:
  0.6 0.7 convert_element_type.17
  1.3 0.7 convert_element_type.16
  1.9 0.1 broadcast_in_dim.12
  2.0 0.7 stack.10
  2.8 0.7 stack.9
  3.5 0.7 tile.12.meta_ref
  4.2 0.7 broadcast_in_dim.13.len_ref
  4.9 0.7 broadcast_in_dim.14.id_ref
  5.6 13.4 %shard_map.50.own_ref = bf16[2,4,256,1024]{3,2,1,0:T(8,128)(2,1)} custom-call(s32[64]{0:T(128)} %len_ref.1, bf16[64,32,1024]{2,1,0:T(8,128)(2,1)} %emb_ref.1), custom_call_target="tpu_custom_call" | custom-call | tf_op jit(solution)/shard_map/pallas_call | solution.py:39
  18.9 114.6 %shard_map.51 = (f32[64,704]{1,0:T(8,128)}, f32[1,64]{1,0:T(1,128)}) custom-call(f32[2,32,128]{2,1,0:T(8,128)} %broadcast_in_dim.13.len_ref, f32[64,128]{1,0:T(8,128)} %broadcast_in_dim.14.id_ref, f32[2,8,128]{2,1,0:T(8,128)} %tile.12.meta_ref, bf16[2,4,256,1024]{3,2,1,0:T(8,128)(2,1)} %shard_map.50.own_ref), custom_call_target="tpu_custom_call" | custom-call | tf_op jit(solution)/shard_map/pallas_call | solution.py:352
  133.6 1.6 %copy.10 = f32[64,704]{1,0:T(8,128)} copy(f32[64,704]{1,0:T(8,128)} %get-tuple-element.8) | data formatting | bytes 360448
  135.2 1.1 copy.11
  (3 shorter events, 0.0 us)

commit v2 on v0

v2 whole, which is shorter than its diff:
```python
import jax
import jax.numpy as jnp
from jax import lax
from jax.experimental import pallas as pl
from jax.experimental.pallas import tpu as pltpu
from jax.sharding import PartitionSpec as P

BLOCK_REACH = 5
TOK = 32
HALF = 32
D = 1024
ROWS = TOK * HALF
GROUP = 16
CHUNK = 256
CHUNKS = ROWS // CHUNK
PIECE = 128
PIECES = ROWS // PIECE
MESH = pl.DeviceIdType.MESH
OFFSETS = ((4, 5, -2, -1, 1), (4, 3, -2, -3, 1), (-4, -3, -2, -5, 1), (-4, -5, -2, 5, -3))


def taken_offsets(role):
    found = []
    for k in range(5):
        for other in range(4):
            if (other + OFFSETS[other][k]) % 4 == role:
                found.append(-OFFSETS[other][k])
    return found


def prep_kernel(len_ref, lens_ref, ids_ref, emb_ref, out_ref, len_rows_ref, id_rows_ref, meta_ref, tmp):
    h, q = pl.program_id(0), pl.program_id(1)
    pos = lax.broadcasted_iota(jnp.int32, (TOK, 1), 0)

    def one(s, carry):
        x = emb_ref[s].astype(jnp.float32)
        ms = jnp.sum(x * x, axis=1, keepdims=True) * (1.0 / D)
        y = x * (lax.rsqrt(ms + 1e-06) * (1.0 / 32.0))
        n = len_ref[h * HALF + q * GROUP + s]
        y = jnp.where(pos < n, y, y[0:1, :])
        for k in range(D // 128):
            tmp[pl.ds(pl.multiple_of(k * GROUP * TOK + s * TOK, TOK), TOK), :] = y[:, k * 128:(k + 1) * 128]
        return carry

    lax.fori_loop(0, GROUP, one, 0, unroll=4)
    for t in range(TOK):
        row = pl.multiple_of(t % 4 * HALF + q * GROUP, GROUP)
        for k in range(D // 128):
            rows = tmp[pl.ds(k * GROUP * TOK + t, GROUP, stride=TOK), :]
            out_ref[t // 4, pl.ds(row, GROUP), k * 128:(k + 1) * 128] = rows.astype(jnp.bfloat16)

    @pl.when((h == 0) & (q == 0))
    def _():
        lane = lax.broadcasted_iota(jnp.int32, (1, 128), 1)
        even = lane // HALF % 2 == 0
        for ref, rows_ref, at in ((lens_ref, len_rows_ref, 0), (ids_ref, id_rows_ref, 4)):
            line = ref[...].astype(jnp.float32)
            rows_ref[...] = jnp.broadcast_to(line, (128, 64)).T
            twice = jnp.concatenate([line, line], axis=1)
            turned = pltpu.roll(twice, HALF, 1)
            meta_ref[0, at:at + 4, :] = jnp.broadcast_to(jnp.where(even, twice, turned), (4, 128))
            meta_ref[1, at:at + 4, :] = jnp.broadcast_to(jnp.where(even, turned, twice), (4, 128))


def prep(emb, lengths, ids):
    whole = lambda shape: pl.BlockSpec(shape, lambda h, q: (0,) * len(shape))
    f32 = jnp.float32
    return pl.pallas_call(
        prep_kernel,
        grid=(2, HALF // GROUP),
        in_specs=[
            pl.BlockSpec(memory_space=pltpu.SMEM),
            whole((1, 64)),
            whole((1, 64)),
            pl.BlockSpec((GROUP, TOK, D), lambda h, q: (h * (HALF // GROUP) + q, 0, 0)),
        ],
        out_specs=[pl.BlockSpec((None, PIECES, PIECE, D), lambda h, q: (h, 0, 0, 0)),
                   whole((64, 128)), whole((64, 128)), whole((2, 8, 128))],
        out_shape=[jax.ShapeDtypeStruct((2, PIECES, PIECE, D), jnp.bfloat16), jax.ShapeDtypeStruct((64, 128), f32),
                   jax.ShapeDtypeStruct((64, 128), f32), jax.ShapeDtypeStruct((2, 8, 128), f32)],
        scratch_shapes=[pltpu.VMEM((GROUP * TOK * D // 128, 128), f32)],
    )(lengths, lengths.reshape(1, 64), ids.reshape(1, 64), emb)


def score_chunk(own_ref, cols, best_ref, row_best_ref, slot, n):
    for h in range(2):
        s = lax.dot_general(own_ref[h].reshape(ROWS, D), cols,
                            (((1,), (1,)), ((), ())), preferred_element_type=jnp.float32)
        row_best_ref[slot, h, n] = jnp.max(s.reshape(TOK, HALF, CHUNK), axis=0)
        cb = s[:, 0:128]
        for k in range(1, CHUNK // 128):
            cb = jnp.maximum(cb, s[:, k * 128:(k + 1) * 128])
        best_ref[slot, h] = jnp.maximum(best_ref[slot, h], cb)


def finish_scores(len_ref, id_ref, meta, best_ref, row_best_ref, slot, x_ref, t_ref):
    lane = lax.broadcasted_iota(jnp.int32, (1, 128), 1)
    col_len = meta[0:1, :]
    scores = []
    for h in range(2):
        row_len = len_ref[h * HALF:(h + 1) * HALF, :]

        def add(t, total):
            b = best_ref[slot, h, pl.ds(pl.multiple_of(t * HALF, HALF), HALF), :]
            b = jnp.maximum(b, pltpu.roll(b, 64, 1))
            b = jnp.maximum(b, pltpu.roll(b, 32, 1))
            return total + jnp.where(row_len > t.astype(jnp.float32), b, 0.0)

        precision = lax.fori_loop(0, TOK, add, jnp.zeros((HALF, 128), jnp.float32), unroll=8) / row_len
        rec = jnp.zeros((HALF, 128), jnp.float32)
        for n in range(CHUNKS):
            for k in range(CHUNK // 128):
                u = (lane // HALF + 4 * (n * (CHUNK // 128) + k)).astype(jnp.float32)
                rec = rec + jnp.where(u < col_len, row_best_ref[slot, h, n, :, k * 128:(k + 1) * 128], 0.0)
        rec = rec + pltpu.roll(rec, 64, 1)
        rec = rec + pltpu.roll(rec, 32, 1)
        recall = rec / col_len
        score = 2.0 * precision * recall / jnp.maximum(precision + recall, 0.5)
        x_ref[slot, h * HALF:(h + 1) * HALF, :] = score
        scores.append(score)
    x_ref[slot, 64:72, :] = jnp.broadcast_to(meta[4:5, :], (8, 128))
    t_ref[slot] = jnp.concatenate(scores + [id_ref[...]], axis=0).T[0:HALF, :]


def main_kernel(len_ref, id_ref, meta_ref, own_ref, x_out, t_out,
                vis, metas, best, row_best, x_mine, x_other, t_mine, t_got,
                send_sem, recv_sem, self_sem, meta_send, meta_recv, x_send, x_recv, t_send, t_recv):
    n_loop = lax.axis_size("loop")
    b, r = lax.axis_index("loop"), lax.axis_index("rep")
    other = 1 - r
    role = b % 4
    half, core = role // 2, role % 2
    early = 5 - 2 * half
    late = 8 - early
    partner = b + 1 - 2 * core

    def block(d):
        return (b + n_loop + d) % n_loop

    def by_role(values):
        v = values
        return v[0] * (1 - half) * (1 - core) + v[1] * (1 - half) * core + v[2] * half * (1 - core) + v[3] * half * core

    def copy(src, dst, ssem, rsem, blk, rp):
        return pltpu.make_async_remote_copy(src_ref=src, dst_ref=dst, send_sem=ssem, recv_sem=rsem,
                                            device_id={"loop": blk, "rep": rp}, device_id_type=MESH)

    barrier = pltpu.get_barrier_semaphore()
    peers = [(block(d), rp) for d in range(-BLOCK_REACH, BLOCK_REACH + 1) if d for rp in (r, other)]
    peers += [(b, other)]
    for blk, rp in peers:
        pl.semaphore_signal(barrier, inc=1, device_id={"loop": blk, "rep": rp}, device_id_type=MESH)
    to_self = pltpu.make_async_copy(own_ref.at[r], vis.at[6], self_sem)
    to_self.start()
    metas[0] = meta_ref[r]

    def clear(i, carry):
        best[i // 2, i % 2] = jnp.full((ROWS, 128), -4.0, jnp.float32)
        return carry

    lax.fori_loop(0, 12, clear, 0)
    pl.semaphore_wait(barrier, len(peers))

    def move(kind, f, src, slot, blk, rp):
        return copy(src, vis.at[slot, f], send_sem.at[kind, f], recv_sem.at[slot, f], blk, rp)

    def arrived(slot, f):
        copy(vis.at[slot, f], vis.at[slot, f], send_sem.at[0, f], recv_sem.at[slot, f], partner, r).wait_recv()

    mine = own_ref.at[r]
    cross = own_ref.at[other]
    starts = {
        0: [(0, mine, 1, block(-4), r), (2, mine, 3, block(2), r)],
        1: [(0, mine, 1, block(-4), r), (4, mine, 5, block(-1), r), (5, mine, 0, block(4), r), (2, cross, 3, block(2), other)],
        2: [(0, mine, 1, block(4), r), (4, cross, 5, block(-1), other)],
        3: [(0, mine, 1, block(4), r), (4, mine, 5, block(-1), r)],
    }

    def first_moves(me, then):
        def one(f, carry):
            for kind, src, slot, blk, rp in starts[me]:
                then(move(kind, f, src.at[f], slot, blk, rp))
            return carry

        lax.fori_loop(0, PIECES, one, 0)

    for me in range(4):
        @pl.when(role == me)
        def _(me=me):
            first_moves(me, lambda c: c.start())

    def meta_copy(k):
        blk = block(by_role([taken_offsets(me)[k] for me in range(4)]))
        return copy(meta_ref.at[r], metas.at[k + 1], meta_send.at[k], meta_recv.at[k], blk, r)

    for k in range(5):
        meta_copy(k).start()

    def after_early(f):
        return [(2, 7, vis.at[3, f], 5, block(1), r), (2, 3, vis.at[3, f], 0, block(-3), r)]

    def after_first(f):
        return [(0, 1, vis.at[1, f], 2, partner, r), (1, 1, vis.at[1, f], 2, partner, r),
                (2, 1, vis.at[1, f], 2, partner, r), (3, 1, vis.at[1, f], 2, partner, r),
                (2, 2, vis.at[1, f], 3, block(-2), r), (3, 2, vis.at[1, f], 3, block(-2), r)]

    def after_relay(f):
        return [(1, 6, vis.at[0, f], 4, block(1), r), (3, 6, vis.at[0, f], 4, block(-4), r)]

    def after_late(f):
        return [(0, 3, vis.at[3, f], 4, partner, r), (1, 3, vis.at[3, f], 4, partner, r)]

    def forward(list_of, f):
        for me in range(4):
            todo = [x for x in list_of(f) if x[0] == me]
            if todo:
                @pl.when(role == me)
                def _(todo=todo):
                    for _, kind, src, slot, blk, rp in todo:
                        move(kind, f, src, slot, blk, rp).start()

    def results(slot):
        out = [copy(x_mine.at[slot], x_other.at[slot], x_send.at[slot], x_recv.at[slot], b, other)]
        if slot:
            blk = block(by_role([OFFSETS[me][slot - 1] for me in range(4)]))
            for i, rp in enumerate((r, other)):
                out.append(copy(t_mine.at[slot], t_got.at[r, slot], t_send.at[i, slot], t_recv.at[r, slot], blk, rp))
        return out

    def send_results(slot):
        for c in results(slot):
            c.start()

    def send_either(one, two):
        pl.when(half == 0)(lambda: send_results(one))
        pl.when(half == 1)(lambda: send_results(two))

    def step(f, carry):
        odd = f % 2

        @pl.when(f < PIECES)
        def _():
            arrived(early, f)
            forward(after_early, f)
            arrived(1, f)
            forward(after_first, f)

            @pl.when(core == 1)
            def _():
                arrived(0, f)
                forward(after_relay, f)

        @pl.when(f > 0)
        def _():
            arrived(late, f - 1)
            forward(after_late, f - 1)

        @pl.when(f == PIECES - 1)
        def _():
            for k in range(5):
                copy(metas.at[k + 1], metas.at[k + 1], meta_send.at[k], meta_recv.at[k], partner, r).wait_recv()

        def part(i, carry):
            slot = odd * (early * (1 - i) + i) + (1 - odd) * ((1 - i) * (2 - i) + late * i * (2 - i) + 2 * i * (i - 1))
            n = (f - 1) // 2

            @pl.when((1 - odd) * (i - 1) != 0)
            def _():
                arrived(slot, 2 * n)
                arrived(slot, 2 * n + 1)

            @pl.when((f == PIECES) & (i == 0))
            def _():
                send_results(0)
                send_either(5, 3)
                send_results(1)

            @pl.when((f == PIECES) & (i == 1))
            def _():
                send_results(2)

            @pl.when((f == PIECES) & (i == 2))
            def _():
                send_either(3, 5)

            scored(slot, slot, n)
            return carry

        @pl.when(f > 0)
        def _():
            lax.fori_loop(0, 3 - odd, part, 0)
        return carry

    def scored(slot, source, n):
        cols = vis[source, pl.ds(2 * n, 2)].reshape(CHUNK, D)
        score_chunk(own_ref, cols, best, row_best, slot, n)

        @pl.when(n == CHUNKS - 1)
        def _():
            finish_scores(len_ref, id_ref, metas[slot], best, row_best, slot, x_mine, t_mine)

    to_self.wait()

    def self_step(n, carry):
        scored(0, 6, n)
        return carry

    lax.fori_loop(0, CHUNKS, self_step, 0)
    lax.fori_loop(0, PIECES + 1, step, 0)

    for slot in range(6):
        x_out[r, slot] = x_mine[slot]
    send_results(4)
    for slot in range(6):
        copy(x_mine.at[slot], x_other.at[slot], x_send.at[slot], x_recv.at[slot], b, other).wait_recv()
        x_out[other, slot] = x_other[slot]
    for slot in range(1, 6):
        for i in range(2):
            copy(t_mine.at[slot], t_got.at[i, slot], t_send.at[i, slot], t_recv.at[i, slot], b, other).wait_recv()
            t_out[i, slot - 1] = t_got[i, slot]

    for slot in range(6):
        for c in results(slot):
            c.wait_send()
    for k in range(5):
        meta_copy(k).wait_send()
    for me in range(4):
        @pl.when(role == me)
        def _(me=me):
            first_moves(me, lambda c: c.wait_send())

            def rest(f, carry):
                for list_of in (after_early, after_first, after_relay, after_late):
                    for who, kind, src, slot, blk, rp in list_of(f):
                        if who == me:
                            move(kind, f, src, slot, blk, rp).wait_send()
                return carry

            lax.fori_loop(0, PIECES, rest, 0)


def place_kernel(role_ref, id_ref, x_ref, t_ref, table_ref, sum_ref):
    role = role_ref[0]
    lane = lax.broadcasted_iota(jnp.int32, (64, 128), 1)
    row = lax.broadcasted_iota(jnp.int32, (64, 128), 0)
    low = lane < 64
    first = (lane % 64) < 32
    ids = id_ref[...]

    def own(k):
        vals = jnp.where(first, x_ref[0, k, 0:64, :], x_ref[1, k, 0:64, :])
        theirs = jnp.where(first[0:8], x_ref[0, k, 64:72, :], x_ref[1, k, 64:72, :])
        return vals, jnp.concatenate([theirs] * 8, axis=0)

    def taken(k, upper):
        both = jnp.concatenate([t_ref[0, k], t_ref[1, k]], axis=0)
        turned = pltpu.roll(both, 64, 1)
        return (turned, both) if upper else (both, turned)

    for mine in range(4):
        @pl.when(role == mine)
        def _(mine=mine):
            taken_at = taken_offsets(mine)
            total = jnp.zeros((64, 128), jnp.float32)
            for p in range(6):
                parts = []
                for upper in range(2):
                    d = 2 * p + upper - BLOCK_REACH
                    if d > BLOCK_REACH:
                        parts.append(parts[0])
                        continue
                    if d == 0:
                        vals, theirs = own(0)
                        same = (theirs == ids) & ((lane % 64) != row)
                    else:
                        if d in OFFSETS[mine]:
                            vals, theirs = own(1 + OFFSETS[mine].index(d))
                        else:
                            vals, theirs = taken(taken_at.index(d), upper)
                        same = theirs == ids
                    inside = (lane >= 64) if upper else low
                    total = total + jnp.where(same & inside, vals, 0.0)
                    parts.append(vals)
                tile = jnp.where(low, parts[0], parts[1])
                width = 128 if p < 5 else 64
                table_ref[:, p * 128:p * 128 + width] = tile[:, 0:width]
            sums = jnp.sum(total, axis=1, keepdims=True)
            sum_ref[...] = jnp.broadcast_to(sums, (64, 128)).T[0:1, :]


def shards(embeddings, lengths, candidate_ids):
    own, len_rows, id_rows, meta = prep(embeddings, lengths, candidate_ids)
    vmem, dma, f32 = pltpu.VMEM, pltpu.SemaphoreType.DMA, jnp.float32
    in_vmem = pl.BlockSpec(memory_space=pltpu.VMEM)
    x, t = pl.pallas_call(
        main_kernel,
        in_specs=[in_vmem] * 4,
        out_specs=[in_vmem] * 2,
        out_shape=[jax.ShapeDtypeStruct((2, 6, 72, 128), f32), jax.ShapeDtypeStruct((2, 5, HALF, 128), f32)],
        scratch_shapes=[
            vmem((7, PIECES, PIECE, D), jnp.bfloat16),
            vmem((6, 8, 128), f32),
            vmem((6, 2, ROWS, 128), f32),
            vmem((6, 2, CHUNKS, HALF, CHUNK), f32),
            vmem((6, 72, 128), f32),
            vmem((6, 72, 128), f32),
            vmem((6, HALF, 128), f32),
            vmem((2, 6, HALF, 128), f32),
            dma((8, PIECES)),
            dma((6, PIECES)),
            dma,
            dma((5,)),
            dma((5,)),
            dma((6,)),
            dma((6,)),
            dma((2, 6)),
            dma((2, 6)),
        ],
        compiler_params=pltpu.CompilerParams(collective_id=0, has_side_effects=True, vmem_limit_bytes=56 << 20),
    )(len_rows, id_rows, meta, own)
    role = (lax.axis_index("loop") % 4).astype(jnp.int32).reshape(1)
    table, sums = pl.pallas_call(
        place_kernel,
        in_specs=[pl.BlockSpec(memory_space=pltpu.SMEM)] + [in_vmem] * 3,
        out_specs=[in_vmem] * 2,
        out_shape=[jax.ShapeDtypeStruct((64, 704), f32), jax.ShapeDtypeStruct((1, 64), f32)],
    )(role, id_rows, x, t)
    return table, sums.reshape(64)


def solution(mesh):
    placed = (P("loop", None, None), P("loop"), P("loop"))
    return jax.shard_map(
        shards, mesh=mesh, in_specs=placed, out_specs=(P("loop", None), P("loop")), check_vma=False
    )
```

time: 242 us -> 103 us (0.43)
  waiting for transfers between devices: 164 us -> 0 us
  Pallas kernels: 21.1 us -> 102 us
  local copies, waits for them, and re-layouts: 37.6 us -> 0 us
  starting transfers between devices: 13.6 us -> 0 us
  other arithmetic: 3.66 us -> 0 us
    ppermute x12 -> x0, waiting for transfers between devices: 164 us -> none  [the longest x10 155 us: move(): return lax.ppermute(value, 'loop', pairs)]
    pallas_call x2, Pallas kernels: 7.68 us -> 90.2 us  [the longest x1 88.2 us: shards(): pl.pallas_call(main_kernel, in_specs=[in_vmem] * 4, out_specs=[in_vmem] *...]
    pallas_call x5 -> x0, local copies, waits for them, and re-layouts: 32.9 us -> none  [score(): pl.pallas_call(score_kernel, in_specs=[pl.BlockSpec(memory_space=pltpu.VM...]
    ppermute x12 -> x0, starting transfers between devices: 13.6 us -> none  [the longest x10 9.98 us: move(): return lax.ppermute(value, 'loop', pairs)]
  transfers between devices with their start and end apart: 12 -> 0, of which waited for: 8 -> 0; matrix products, arithmetic and copies ran while one was open for 14% -> 0% of each run, Pallas kernels for 2% -> 0%
where the time goes in v2:
time: 103 us
  Pallas kernels  102 us (99%)
    pallas_call x1, Pallas kernels, shards(): pl.pallas_call(main_kernel, in_specs=[in_vmem] * 4, out_specs=[in_vmem] *...  88.2 us
    pallas_call x1, Pallas kernels, prep(): pl.pallas_call(prep_kernel, grid=(2, HALF // GROUP), in_specs=[pl.BlockSp...  12.2 us

profile of v2, /device:TPU:0, one launch (start us, length us, event | category | flops | bytes accessed | tf_op | source)
XLA Modules:
  0.0 103.0 jit_solution(4783487966587687325)
XLA Ops:
  0.6 12.2 %shard_map.50 = (bf16[2,8,128,1024]{3,2,1,0:T(8,128)(2,1)}, f32[64,128]{1,0:T(8,128)}, f32[64,128]{1,0:T(8,128)}, f32[2,8,128]{2,1,0:T(8,128)}) custom-call(s32[64]{0:T(128)} %len_ref.1, s32[1,64]{1,0:T(1,128)} %bitcast.4, s32[1,64]{1,0:T(1,128)} %bitcast.5, bf16[64,32,1024]{2,1,0:T(8,128)(2,1)} %emb_ref.1), custom_call_target="tpu_custom_call" | custom-call | tf_op jit(solution)/shard_map/pallas_call | solution.py:68
  12.9 88.2 %shard_map.51 = (f32[2,6,72,128]{3,2,1,0:T(8,128)}, f32[2,5,32,128]{3,2,1,0:T(8,128)}) custom-call(f32[64,128]{1,0:T(8,128)} %get-tuple-element.11.len_ref, f32[64,128]{1,0:T(8,128)} %get-tuple-element.10.id_ref, f32[2,8,128]{2,1,0:T(8,128)} %get-tuple-element.12.meta_ref, bf16[2,8,128,1024]{3,2,1,0:T(8,128)(2,1)} %get-tuple-element.13.own_ref), custom_call_target="tpu_custom_call" | custom-call | tf_op jit(solution)/shard_map/pallas_call | solution.py:395
  101.1 2.0 %shard_map.52 = (f32[64,704]{1,0:T(8,128)}, f32[1,64]{1,0:T(1,128)}) custom-call(s32[1]{0:T(128)} %bitcast.role_ref, f32[64,128]{1,0:T(8,128)} %get-tuple-element.10.id_ref, f32[2,6,72,128]{3,2,1,0:T(8,128)} %get-tuple-element.14.x_ref, f32[2,5,32,128]{3,2,1,0:T(8,128)} %get-tuple-element.15.t_ref), custom_call_target="tpu_custom_call" | custom-call | tf_op jit(solution)/shard_map/pallas_call | solution.py:422

commit v3 on v2

--- a/solution.py
+++ b/solution.py
@@ -13,8 +13,7 @@
 GROUP = 16
 CHUNK = 256
 CHUNKS = ROWS // CHUNK
-PIECE = 128
-PIECES = ROWS // PIECE
+PIECES = 8
 MESH = pl.DeviceIdType.MESH
 OFFSETS = ((4, 5, -2, -1, 1), (4, 3, -2, -3, 1), (-4, -3, -2, -5, 1), (-4, -5, -2, 5, -3))
 
@@ -28,58 +27,31 @@
     return found
 
 
-def prep_kernel(len_ref, lens_ref, ids_ref, emb_ref, out_ref, len_rows_ref, id_rows_ref, meta_ref, tmp):
-    h, q = pl.program_id(0), pl.program_id(1)
-    pos = lax.broadcasted_iota(jnp.int32, (TOK, 1), 0)
-
-    def one(s, carry):
-        x = emb_ref[s].astype(jnp.float32)
-        ms = jnp.sum(x * x, axis=1, keepdims=True) * (1.0 / D)
-        y = x * (lax.rsqrt(ms + 1e-06) * (1.0 / 32.0))
-        n = len_ref[h * HALF + q * GROUP + s]
-        y = jnp.where(pos < n, y, y[0:1, :])
-        for k in range(D // 128):
-            tmp[pl.ds(pl.multiple_of(k * GROUP * TOK + s * TOK, TOK), TOK), :] = y[:, k * 128:(k + 1) * 128]
-        return carry
-
-    lax.fori_loop(0, GROUP, one, 0, unroll=4)
-    for t in range(TOK):
-        row = pl.multiple_of(t % 4 * HALF + q * GROUP, GROUP)
-        for k in range(D // 128):
-            rows = tmp[pl.ds(k * GROUP * TOK + t, GROUP, stride=TOK), :]
-            out_ref[t // 4, pl.ds(row, GROUP), k * 128:(k + 1) * 128] = rows.astype(jnp.bfloat16)
-
-    @pl.when((h == 0) & (q == 0))
-    def _():
-        lane = lax.broadcasted_iota(jnp.int32, (1, 128), 1)
-        even = lane // HALF % 2 == 0
-        for ref, rows_ref, at in ((lens_ref, len_rows_ref, 0), (ids_ref, id_rows_ref, 4)):
-            line = ref[...].astype(jnp.float32)
-            rows_ref[...] = jnp.broadcast_to(line, (128, 64)).T
-            twice = jnp.concatenate([line, line], axis=1)
-            turned = pltpu.roll(twice, HALF, 1)
-            meta_ref[0, at:at + 4, :] = jnp.broadcast_to(jnp.where(even, twice, turned), (4, 128))
-            meta_ref[1, at:at + 4, :] = jnp.broadcast_to(jnp.where(even, turned, twice), (4, 128))
-
-
-def prep(emb, lengths, ids):
-    whole = lambda shape: pl.BlockSpec(shape, lambda h, q: (0,) * len(shape))
-    f32 = jnp.float32
-    return pl.pallas_call(
-        prep_kernel,
-        grid=(2, HALF // GROUP),
-        in_specs=[
-            pl.BlockSpec(memory_space=pltpu.SMEM),
-            whole((1, 64)),
-            whole((1, 64)),
-            pl.BlockSpec((GROUP, TOK, D), lambda h, q: (h * (HALF // GROUP) + q, 0, 0)),
-        ],
-        out_specs=[pl.BlockSpec((None, PIECES, PIECE, D), lambda h, q: (h, 0, 0, 0)),
-                   whole((64, 128)), whole((64, 128)), whole((2, 8, 128))],
-        out_shape=[jax.ShapeDtypeStruct((2, PIECES, PIECE, D), jnp.bfloat16), jax.ShapeDtypeStruct((64, 128), f32),
-                   jax.ShapeDtypeStruct((64, 128), f32), jax.ShapeDtypeStruct((2, 8, 128), f32)],
-        scratch_shapes=[pltpu.VMEM((GROUP * TOK * D // 128, 128), f32)],
-    )(lengths, lengths.reshape(1, 64), ids.reshape(1, 64), emb)
+def rows_of(line):
+    return jnp.broadcast_to(line.astype(jnp.float32), (128, 64)).T
+
+
+def turned_tokens():
+    out = lax.broadcasted_iota(jnp.int32, (256, 256), 0)
+    into = lax.broadcasted_iota(jnp.int32, (256, 256), 1)
+    hit = (out // 16 == into % 16) & (out % 16 == into // 16)
+    return jnp.where(hit, 1.0, 0.0).astype(jnp.bfloat16)
+
+
+def prepare(emb, turn, lens, put):
+    first = None
+    for g in range(TOK // 16):
+        raw = emb[:, g * 16:(g + 1) * 16, :].reshape(256, D)
+        x = jnp.dot(turn, raw, preferred_element_type=jnp.float32)
+        for t in range(16):
+            rows = x[t * GROUP:(t + 1) * GROUP, :]
+            ms = jnp.sum(rows * rows, axis=1, keepdims=True) * (1.0 / D)
+            rows = rows * (lax.rsqrt(ms + 1e-06) * (1.0 / 32.0))
+            if first is None:
+                first = rows
+            else:
+                rows = jnp.where(lens > float(g * 16 + t), rows, first)
+            put(g * 16 + t, rows.astype(jnp.bfloat16))
 
 
 def score_chunk(own_ref, cols, best_ref, row_best_ref, slot, n):
@@ -122,9 +94,9 @@
     t_ref[slot] = jnp.concatenate(scores + [id_ref[...]], axis=0).T[0:HALF, :]
 
 
-def main_kernel(len_ref, id_ref, meta_ref, own_ref, x_out, t_out,
-                vis, metas, best, row_best, x_mine, x_other, t_mine, t_got,
-                send_sem, recv_sem, self_sem, meta_send, meta_recv, x_send, x_recv, t_send, t_recv):
+def main_kernel(lens_ref, ids_ref, emb_ref, x_out, t_out,
+                raw, turn, own_ref, len_ref, id_ref, meta_ref, vis, metas, best, row_best, x_mine, x_other, t_mine, t_got,
+                raw_sem, send_sem, recv_sem, self_sem, meta_send, meta_recv, x_send, x_recv, t_send, t_recv):
     n_loop = lax.axis_size("loop")
     b, r = lax.axis_index("loop"), lax.axis_index("rep")
     other = 1 - r
@@ -145,14 +117,41 @@
         return pltpu.make_async_remote_copy(src_ref=src, dst_ref=dst, send_sem=ssem, recv_sem=rsem,
                                             device_id={"loop": blk, "rep": rp}, device_id_type=MESH)
 
+    def fetch(g):
+        base = (r + (1 - 2 * r) * (g // 2)) * HALF + g % 2 * GROUP
+        return pltpu.make_async_copy(emb_ref.at[pl.ds(base, GROUP)], raw.at[g], raw_sem.at[g])
+
+    for g in range(4):
+        fetch(g).start()
     barrier = pltpu.get_barrier_semaphore()
     peers = [(block(d), rp) for d in range(-BLOCK_REACH, BLOCK_REACH + 1) if d for rp in (r, other)]
     peers += [(b, other)]
     for blk, rp in peers:
         pl.semaphore_signal(barrier, inc=1, device_id={"loop": blk, "rep": rp}, device_id_type=MESH)
-    to_self = pltpu.make_async_copy(own_ref.at[r], vis.at[6], self_sem)
-    to_self.start()
+    turn[...] = turned_tokens()
+    lane = lax.broadcasted_iota(jnp.int32, (1, 128), 1)
+    even = lane // HALF % 2 == 0
+    for ref, rows_ref, at in ((lens_ref, len_ref, 0), (ids_ref, id_ref, 4)):
+        rows_ref[...] = rows_of(ref[...])
+        line = ref[...].astype(jnp.float32)
+        twice = jnp.concatenate([line, line], axis=1)
+        rolled = pltpu.roll(twice, HALF, 1)
+        meta_ref[0, at:at + 4, :] = jnp.broadcast_to(jnp.where(even, twice, rolled), (4, 128))
+        meta_ref[1, at:at + 4, :] = jnp.broadcast_to(jnp.where(even, rolled, twice), (4, 128))
     metas[0] = meta_ref[r]
+
+    def prepare_group(g, carry):
+        h, q = r + (1 - 2 * r) * (g // 2), g % 2
+        fetch(g).wait()
+
+        def put(t, rows):
+            own_ref[h, t // 4, t % 4, q] = rows
+
+        lens = len_ref[pl.ds(pl.multiple_of(h * HALF + q * GROUP, GROUP), GROUP), :][:, 0:1]
+        prepare(raw.at[g], turn[...], lens, put)
+        return carry
+
+    lax.fori_loop(0, 2, prepare_group, 0)
 
     def clear(i, carry):
         best[i // 2, i % 2] = jnp.full((ROWS, 128), -4.0, jnp.float32)
@@ -171,23 +170,25 @@
     cross = own_ref.at[other]
     starts = {
         0: [(0, mine, 1, block(-4), r), (2, mine, 3, block(2), r)],
-        1: [(0, mine, 1, block(-4), r), (4, mine, 5, block(-1), r), (5, mine, 0, block(4), r), (2, cross, 3, block(2), other)],
-        2: [(0, mine, 1, block(4), r), (4, cross, 5, block(-1), other)],
+        1: [(0, mine, 1, block(-4), r), (4, mine, 5, block(-1), r), (5, mine, 0, block(4), r)],
+        2: [(0, mine, 1, block(4), r)],
         3: [(0, mine, 1, block(4), r), (4, mine, 5, block(-1), r)],
     }
-
-    def first_moves(me, then):
+    crossing = {0: [], 1: [(2, cross, 3, block(2), other)], 2: [(4, cross, 5, block(-1), other)], 3: []}
+
+    def first_moves(me, lists, then):
         def one(f, carry):
-            for kind, src, slot, blk, rp in starts[me]:
+            for kind, src, slot, blk, rp in lists[me]:
                 then(move(kind, f, src.at[f], slot, blk, rp))
             return carry
 
-        lax.fori_loop(0, PIECES, one, 0)
+        if lists[me]:
+            lax.fori_loop(0, PIECES, one, 0)
 
     for me in range(4):
         @pl.when(role == me)
         def _(me=me):
-            first_moves(me, lambda c: c.start())
+            first_moves(me, starts, lambda c: c.start())
 
     def meta_copy(k):
         blk = block(by_role([taken_offsets(me)[k] for me in range(4)]))
@@ -195,6 +196,9 @@
 
     for k in range(5):
         meta_copy(k).start()
+    to_self = pltpu.make_async_copy(own_ref.at[r], vis.at[6], self_sem)
+    to_self.start()
+    lax.fori_loop(2, 4, prepare_group, 0)
 
     def after_early(f):
         return [(2, 7, vis.at[3, f], 5, block(1), r), (2, 3, vis.at[3, f], 0, block(-3), r)]
@@ -298,6 +302,11 @@
         @pl.when(n == CHUNKS - 1)
         def _():
             finish_scores(len_ref, id_ref, metas[slot], best, row_best, slot, x_mine, t_mine)
+
+    for me in range(4):
+        @pl.when(role == me)
+        def _(me=me):
+            first_moves(me, crossing, lambda c: c.start())
 
     to_self.wait()
 
@@ -327,7 +336,8 @@
     for me in range(4):
         @pl.when(role == me)
         def _(me=me):
-            first_moves(me, lambda c: c.wait_send())
+            first_moves(me, starts, lambda c: c.wait_send())
+            first_moves(me, crossing, lambda c: c.wait_send())
 
             def rest(f, carry):
                 for list_of in (after_early, after_first, after_relay, after_late):
@@ -339,13 +349,13 @@
             lax.fori_loop(0, PIECES, rest, 0)
 
 
-def place_kernel(role_ref, id_ref, x_ref, t_ref, table_ref, sum_ref):
+def place_kernel(role_ref, ids_ref, x_ref, t_ref, table_ref, sum_ref):
     role = role_ref[0]
     lane = lax.broadcasted_iota(jnp.int32, (64, 128), 1)
     row = lax.broadcasted_iota(jnp.int32, (64, 128), 0)
     low = lane < 64
     first = (lane % 64) < 32
-    ids = id_ref[...]
+    ids = rows_of(ids_ref[...])
 
     def own(k):
         vals = jnp.where(first, x_ref[0, k, 0:64, :], x_ref[1, k, 0:64, :])
@@ -389,16 +399,22 @@
 
 
 def shards(embeddings, lengths, candidate_ids):
-    own, len_rows, id_rows, meta = prep(embeddings, lengths, candidate_ids)
+    lens, ids = lengths.reshape(1, -1), candidate_ids.reshape(1, -1)
     vmem, dma, f32 = pltpu.VMEM, pltpu.SemaphoreType.DMA, jnp.float32
     in_vmem = pl.BlockSpec(memory_space=pltpu.VMEM)
     x, t = pl.pallas_call(
         main_kernel,
-        in_specs=[in_vmem] * 4,
+        in_specs=[in_vmem, in_vmem, pl.BlockSpec(memory_space=pl.ANY)],
         out_specs=[in_vmem] * 2,
         out_shape=[jax.ShapeDtypeStruct((2, 6, 72, 128), f32), jax.ShapeDtypeStruct((2, 5, HALF, 128), f32)],
         scratch_shapes=[
-            vmem((7, PIECES, PIECE, D), jnp.bfloat16),
+            vmem((4, GROUP, TOK, D), jnp.bfloat16),
+            vmem((256, 256), jnp.bfloat16),
+            vmem((2, PIECES, 4, 2, GROUP, D), jnp.bfloat16),
+            vmem((64, 128), f32),
+            vmem((64, 128), f32),
+            vmem((2, 8, 128), f32),
+            vmem((7, PIECES, 4, 2, GROUP, D), jnp.bfloat16),
             vmem((6, 8, 128), f32),
             vmem((6, 2, ROWS, 128), f32),
             vmem((6, 2, CHUNKS, HALF, CHUNK), f32),
@@ -406,6 +422,7 @@
             vmem((6, 72, 128), f32),
             vmem((6, HALF, 128), f32),
             vmem((2, 6, HALF, 128), f32),
+            dma((4,)),
             dma((8, PIECES)),
             dma((6, PIECES)),
             dma,
@@ -417,14 +434,14 @@
             dma((2, 6)),
         ],
         compiler_params=pltpu.CompilerParams(collective_id=0, has_side_effects=True, vmem_limit_bytes=56 << 20),
-    )(len_rows, id_rows, meta, own)
+    )(lens, ids, embeddings)
     role = (lax.axis_index("loop") % 4).astype(jnp.int32).reshape(1)
     table, sums = pl.pallas_call(
         place_kernel,
         in_specs=[pl.BlockSpec(memory_space=pltpu.SMEM)] + [in_vmem] * 3,
         out_specs=[in_vmem] * 2,
         out_shape=[jax.ShapeDtypeStruct((64, 704), f32), jax.ShapeDtypeStruct((1, 64), f32)],
-    )(role, id_rows, x, t)
+    )(role, ids, x, t)
     return table, sums.reshape(64)
 
 

time: 103 us -> 90.7 us (0.88)
  Pallas kernels: 102 us -> 89.9 us
    pallas_call x2 -> x1, Pallas kernels: 100 us -> 87.8 us  [shards(): pl.pallas_call(main_kernel, in_specs=[in_vmem, in_vmem, pl.BlockSpec(memo...]
where the time goes in v3:
time: 90.7 us; the launch traced here: 90.6 us
  Pallas kernels  89.9 us (99%)
    pallas_call x1, Pallas kernels, shards(): pl.pallas_call(main_kernel, in_specs=[in_vmem, in_vmem, pl.BlockSpec(memo...  87.8 us
    pallas_call x1, Pallas kernels, shards(): pl.pallas_call(place_kernel, in_specs=[pl.BlockSpec(memory_space=pltpu.SM...  2.07 us

profile of v3, /device:TPU:0, one launch (start us, length us, event | category | flops | bytes accessed | tf_op | source)
XLA Modules:
  0.0 90.6 jit_solution(8377220448085501704)
XLA Ops:
  0.6 87.8 %shard_map.50 = (f32[2,6,72,128]{3,2,1,0:T(8,128)}, f32[2,5,32,128]{3,2,1,0:T(8,128)}) custom-call(s32[1,64]{1,0:T(1,128)} %bitcast.6, s32[1,64]{1,0:T(1,128)} %bitcast.4, bf16[64,32,1024]{2,1,0:T(8,128)(2,1)} %emb_ref.1), custom_call_target="tpu_custom_call" | custom-call | tf_op jit(solution)/shard_map/pallas_call | solution.py:405
  88.5 2.1 %shard_map.51 = (f32[64,704]{1,0:T(8,128)}, f32[1,64]{1,0:T(1,128)}) custom-call(s32[1]{0:T(128)} %bitcast.role_ref, s32[1,64]{1,0:T(1,128)} %bitcast.5, f32[2,6,72,128]{3,2,1,0:T(8,128)} %get-tuple-element.6.x_ref, f32[2,5,32,128]{3,2,1,0:T(8,128)} %get-tuple-element.7.t_ref), custom_call_target="tpu_custom_call" | custom-call | tf_op jit(solution)/shard_map/pallas_call | solution.py:439

commit v4 on v3

--- a/solution.py
+++ b/solution.py
@@ -11,9 +11,7 @@
 D = 1024
 ROWS = TOK * HALF
 GROUP = 16
-CHUNK = 256
-CHUNKS = ROWS // CHUNK
-PIECES = 8
+PIECES = 16
 MESH = pl.DeviceIdType.MESH
 OFFSETS = ((4, 5, -2, -1, 1), (4, 3, -2, -3, 1), (-4, -3, -2, -5, 1), (-4, -5, -2, 5, -3))
 
@@ -54,44 +52,46 @@
             put(g * 16 + t, rows.astype(jnp.bfloat16))
 
 
-def score_chunk(own_ref, cols, best_ref, row_best_ref, slot, n):
+def score_piece(own_ref, cols, best_ref, row_best_ref, acc, e):
     for h in range(2):
         s = lax.dot_general(own_ref[h].reshape(ROWS, D), cols,
                             (((1,), (1,)), ((), ())), preferred_element_type=jnp.float32)
-        row_best_ref[slot, h, n] = jnp.max(s.reshape(TOK, HALF, CHUNK), axis=0)
-        cb = s[:, 0:128]
-        for k in range(1, CHUNK // 128):
-            cb = jnp.maximum(cb, s[:, k * 128:(k + 1) * 128])
-        best_ref[slot, h] = jnp.maximum(best_ref[slot, h], cb)
-
-
-def finish_scores(len_ref, id_ref, meta, best_ref, row_best_ref, slot, x_ref, t_ref):
+        row_best_ref[acc, h, e] = jnp.max(s.reshape(TOK, HALF, 256), axis=0)
+        best_ref[acc, h] = jnp.maximum(best_ref[acc, h], jnp.maximum(s[:, 0:128], s[:, 128:256]))
+
+
+def finish_scores(len_ref, id_ref, col_len, col_id, best_ref, row_best_ref, acc, x_ref, t_ref):
+    twice = acc == 0
     lane = lax.broadcasted_iota(jnp.int32, (1, 128), 1)
-    col_len = meta[0:1, :]
     scores = []
     for h in range(2):
         row_len = len_ref[h * HALF:(h + 1) * HALF, :]
 
         def add(t, total):
-            b = best_ref[slot, h, pl.ds(pl.multiple_of(t * HALF, HALF), HALF), :]
-            b = jnp.maximum(b, pltpu.roll(b, 64, 1))
-            b = jnp.maximum(b, pltpu.roll(b, 32, 1))
+            b = best_ref[acc, h, pl.ds(pl.multiple_of(t * HALF, HALF), HALF), :]
+            if twice:
+                b = jnp.maximum(b, pltpu.roll(b, 64, 1))
             return total + jnp.where(row_len > t.astype(jnp.float32), b, 0.0)
 
-        precision = lax.fori_loop(0, TOK, add, jnp.zeros((HALF, 128), jnp.float32), unroll=8) / row_len
-        rec = jnp.zeros((HALF, 128), jnp.float32)
-        for n in range(CHUNKS):
-            for k in range(CHUNK // 128):
-                u = (lane // HALF + 4 * (n * (CHUNK // 128) + k)).astype(jnp.float32)
-                rec = rec + jnp.where(u < col_len, row_best_ref[slot, h, n, :, k * 128:(k + 1) * 128], 0.0)
-        rec = rec + pltpu.roll(rec, 64, 1)
-        rec = rec + pltpu.roll(rec, 32, 1)
+        def add_rows(e, total):
+            for k in range(2):
+                u = (2 * e + k).astype(jnp.float32)
+                if twice:
+                    u = u + jnp.where(lane < 64, 0.0, 16.0)
+                total = total + jnp.where(u < col_len, row_best_ref[acc, h, e, :, k * 128:(k + 1) * 128], 0.0)
+            return total
+
+        zero = jnp.zeros((HALF, 128), jnp.float32)
+        precision = lax.fori_loop(0, TOK, add, zero, unroll=8) / row_len
+        rec = lax.fori_loop(0, PIECES // 2 if twice else PIECES, add_rows, zero, unroll=4)
+        if twice:
+            rec = rec + pltpu.roll(rec, 64, 1)
         recall = rec / col_len
         score = 2.0 * precision * recall / jnp.maximum(precision + recall, 0.5)
-        x_ref[slot, h * HALF:(h + 1) * HALF, :] = score
+        x_ref[acc, h * HALF:(h + 1) * HALF, :] = score
         scores.append(score)
-    x_ref[slot, 64:72, :] = jnp.broadcast_to(meta[4:5, :], (8, 128))
-    t_ref[slot] = jnp.concatenate(scores + [id_ref[...]], axis=0).T[0:HALF, :]
+    x_ref[acc, 64:72, :] = jnp.broadcast_to(col_id, (8, 128))
+    t_ref[acc] = jnp.concatenate(scores + [id_ref[...]], axis=0).T
 
 
 def main_kernel(lens_ref, ids_ref, emb_ref, x_out, t_out,
@@ -102,7 +102,7 @@
     other = 1 - r
     role = b % 4
     half, core = role // 2, role % 2
-    early = 5 - 2 * half
+    early = 5 - 2 * half * core
     late = 8 - early
     partner = b + 1 - 2 * core
 
@@ -145,7 +145,7 @@
         fetch(g).wait()
 
         def put(t, rows):
-            own_ref[h, t // 4, t % 4, q] = rows
+            own_ref[h, t // 2, t % 2, q] = rows
 
         lens = len_ref[pl.ds(pl.multiple_of(h * HALF + q * GROUP, GROUP), GROUP), :][:, 0:1]
         prepare(raw.at[g], turn[...], lens, put)
@@ -157,7 +157,7 @@
         best[i // 2, i % 2] = jnp.full((ROWS, 128), -4.0, jnp.float32)
         return carry
 
-    lax.fori_loop(0, 12, clear, 0)
+    lax.fori_loop(0, 4, clear, 0)
     pl.semaphore_wait(barrier, len(peers))
 
     def move(kind, f, src, slot, blk, rp):
@@ -170,7 +170,7 @@
     cross = own_ref.at[other]
     starts = {
         0: [(0, mine, 1, block(-4), r), (2, mine, 3, block(2), r)],
-        1: [(0, mine, 1, block(-4), r), (4, mine, 5, block(-1), r), (5, mine, 0, block(4), r)],
+        1: [(0, mine, 1, block(-4), r), (4, mine, 5, block(-1), r)],
         2: [(0, mine, 1, block(4), r)],
         3: [(0, mine, 1, block(4), r), (4, mine, 5, block(-1), r)],
     }
@@ -200,22 +200,23 @@
     to_self.start()
     lax.fori_loop(2, 4, prepare_group, 0)
 
-    def after_early(f):
-        return [(2, 7, vis.at[3, f], 5, block(1), r), (2, 3, vis.at[3, f], 0, block(-3), r)]
-
     def after_first(f):
         return [(0, 1, vis.at[1, f], 2, partner, r), (1, 1, vis.at[1, f], 2, partner, r),
                 (2, 1, vis.at[1, f], 2, partner, r), (3, 1, vis.at[1, f], 2, partner, r),
                 (2, 2, vis.at[1, f], 3, block(-2), r), (3, 2, vis.at[1, f], 3, block(-2), r)]
 
+    def after_third(f):
+        return [(0, 3, vis.at[3, f], 4, partner, r), (1, 3, vis.at[3, f], 4, partner, r),
+                (2, 7, vis.at[3, f], 5, block(1), r), (2, 3, vis.at[3, f], 0, block(-3), r)]
+
     def after_relay(f):
-        return [(1, 6, vis.at[0, f], 4, block(1), r), (3, 6, vis.at[0, f], 4, block(-4), r)]
-
-    def after_late(f):
-        return [(0, 3, vis.at[3, f], 4, partner, r), (1, 3, vis.at[3, f], 4, partner, r)]
-
-    def forward(list_of, f):
-        for me in range(4):
+        return [(3, 6, vis.at[0, f], 4, block(-4), r)]
+
+    def ahead(f):
+        return [(1, 5, mine.at[f], 4, block(5), r)]
+
+    def forward(list_of, f, only=range(4)):
+        for me in only:
             todo = [x for x in list_of(f) if x[0] == me]
             if todo:
                 @pl.when(role == me)
@@ -223,85 +224,107 @@
                     for _, kind, src, slot, blk, rp in todo:
                         move(kind, f, src, slot, blk, rp).start()
 
-    def results(slot):
-        out = [copy(x_mine.at[slot], x_other.at[slot], x_send.at[slot], x_recv.at[slot], b, other)]
-        if slot:
-            blk = block(by_role([OFFSETS[me][slot - 1] for me in range(4)]))
-            for i, rp in enumerate((r, other)):
-                out.append(copy(t_mine.at[slot], t_got.at[r, slot], t_send.at[i, slot], t_recv.at[r, slot], blk, rp))
+    def x_copy(acc):
+        return copy(x_mine.at[acc], x_other.at[acc], x_send.at[acc], x_recv.at[acc], b, other)
+
+    def t_copies(acc, v):
+        if acc == 0:
+            slot, picked = early, [2 if me == 3 else 4 for me in range(4)]
+        elif v == 2:
+            slot, picked = late, [4 if me == 3 else 2 for me in range(4)]
+        else:
+            slot, picked = (1, 2, None, 4)[v], [(0, 1, None, 3)[v]] * 4
+        blk = block(by_role([OFFSETS[me][picked[me]] for me in range(4)]))
+        src = t_mine.at[acc, pl.ds(v * HALF, HALF)]
+        sem = 4 if acc == 0 else v
+        return [copy(src, t_got.at[r, slot - 1], t_send.at[i, sem], t_recv.at[r, slot - 1], blk, rp)
+                for i, rp in enumerate((r, other))]
+
+    def results(acc):
+        out = [x_copy(acc)]
+        for v in ((1,) if acc == 0 else range(4)):
+            out += t_copies(acc, v)
         return out
 
-    def send_results(slot):
-        for c in results(slot):
-            c.start()
-
-    def send_either(one, two):
-        pl.when(half == 0)(lambda: send_results(one))
-        pl.when(half == 1)(lambda: send_results(two))
+    group = lax.broadcasted_iota(jnp.int32, (1, 128), 1) // HALF
+
+    def finish(acc):
+        def lanes(at):
+            row = lambda k: metas[k, at:at + 1, :]
+            if acc == 0:
+                return jnp.where(group % 2 == 0, row(0), row(early))
+            return jnp.where(group < 2, jnp.where(group == 0, row(1), row(2)), jnp.where(group == 2, row(late), row(4)))
+
+        finish_scores(len_ref, id_ref, lanes(0), lanes(4), best, row_best, acc, x_mine, t_mine)
 
     def step(f, carry):
-        odd = f % 2
-
         @pl.when(f < PIECES)
         def _():
-            arrived(early, f)
-            forward(after_early, f)
             arrived(1, f)
             forward(after_first, f)
 
-            @pl.when(core == 1)
+            @pl.when(role == 2)
             def _():
-                arrived(0, f)
-                forward(after_relay, f)
-
-        @pl.when(f > 0)
-        def _():
-            arrived(late, f - 1)
-            forward(after_late, f - 1)
-
-        @pl.when(f == PIECES - 1)
+                arrived(3, f)
+                forward(after_third, f, (2,))
+
+        @pl.when((f > 0) & (f <= PIECES))
+        def _():
+            @pl.when(half == 0)
+            def _():
+                arrived(3, f - 1)
+                forward(after_third, f - 1, (0, 1))
+
+            @pl.when(role == 3)
+            def _():
+                arrived(0, f - 1)
+                forward(after_relay, f - 1)
+
+        @pl.when((f >= 3) & (f < 13))
+        def _():
+            forward(ahead, f - 3)
+
+        @pl.when((f >= 13) & (f < PIECES))
+        def _():
+            forward(ahead, 2 * f - 16)
+            forward(ahead, 2 * f - 15)
+
+        def part(i, carry):
+            e = f - 4 + i
+            far = e + 8 * (1 - i)
+
+            @pl.when(i == 0)
+            def _():
+                arrived(early, e)
+                arrived(early, far)
+
+            @pl.when(i == 1)
+            def _():
+                arrived(2, e)
+                arrived(4, e)
+                pl.when(role == 3)(lambda: arrived(5, e))
+
+            slots = (6 - 5 * i, early * (1 - i) + 2 * i, 6 * (1 - i) + late * i, early * (1 - i) + 4 * i)
+            places = (e, e, far, far)
+            cols = jnp.concatenate([vis[slot, at, k].reshape(HALF, D) for k in range(2)
+                                    for slot, at in zip(slots, places)], axis=0)
+            score_piece(own_ref, cols, best, row_best, i, e)
+            return carry
+
+        window = (f + 4) // 8
+        lax.fori_loop(1 - window * (2 - window), 1 + (f + 13) // 16, part, 0)
+
+        @pl.when(f == 12)
         def _():
             for k in range(5):
                 copy(metas.at[k + 1], metas.at[k + 1], meta_send.at[k], meta_recv.at[k], partner, r).wait_recv()
-
-        def part(i, carry):
-            slot = odd * (early * (1 - i) + i) + (1 - odd) * ((1 - i) * (2 - i) + late * i * (2 - i) + 2 * i * (i - 1))
-            n = (f - 1) // 2
-
-            @pl.when((1 - odd) * (i - 1) != 0)
-            def _():
-                arrived(slot, 2 * n)
-                arrived(slot, 2 * n + 1)
-
-            @pl.when((f == PIECES) & (i == 0))
-            def _():
-                send_results(0)
-                send_either(5, 3)
-                send_results(1)
-
-            @pl.when((f == PIECES) & (i == 1))
-            def _():
-                send_results(2)
-
-            @pl.when((f == PIECES) & (i == 2))
-            def _():
-                send_either(3, 5)
-
-            scored(slot, slot, n)
-            return carry
-
-        @pl.when(f > 0)
-        def _():
-            lax.fori_loop(0, 3 - odd, part, 0)
+            finish(0)
+
+        @pl.when(f == 13)
+        def _():
+            for c in results(0):
+                c.start()
         return carry
-
-    def scored(slot, source, n):
-        cols = vis[source, pl.ds(2 * n, 2)].reshape(CHUNK, D)
-        score_chunk(own_ref, cols, best, row_best, slot, n)
-
-        @pl.when(n == CHUNKS - 1)
-        def _():
-            finish_scores(len_ref, id_ref, metas[slot], best, row_best, slot, x_mine, t_mine)
 
     for me in range(4):
         @pl.when(role == me)
@@ -309,27 +332,22 @@
             first_moves(me, crossing, lambda c: c.start())
 
     to_self.wait()
-
-    def self_step(n, carry):
-        scored(0, 6, n)
-        return carry
-
-    lax.fori_loop(0, CHUNKS, self_step, 0)
-    lax.fori_loop(0, PIECES + 1, step, 0)
-
-    for slot in range(6):
-        x_out[r, slot] = x_mine[slot]
-    send_results(4)
-    for slot in range(6):
-        copy(x_mine.at[slot], x_other.at[slot], x_send.at[slot], x_recv.at[slot], b, other).wait_recv()
-        x_out[other, slot] = x_other[slot]
-    for slot in range(1, 6):
+    lax.fori_loop(0, PIECES + 3, step, 0)
+    finish(1)
+    for acc in range(2):
+        x_out[r, acc] = x_mine[acc]
+    for c in results(1):
+        c.start()
+    for acc in range(2):
+        x_copy(acc).wait_recv()
+        x_out[other, acc] = x_other[acc]
+    for k in range(5):
         for i in range(2):
-            copy(t_mine.at[slot], t_got.at[i, slot], t_send.at[i, slot], t_recv.at[i, slot], b, other).wait_recv()
-            t_out[i, slot - 1] = t_got[i, slot]
-
-    for slot in range(6):
-        for c in results(slot):
+            copy(t_got.at[i, k], t_got.at[i, k], t_send.at[i, k], t_recv.at[i, k], b, other).wait_recv()
+            t_out[i, k] = t_got[i, k]
+
+    for acc in range(2):
+        for c in results(acc):
             c.wait_send()
     for k in range(5):
         meta_copy(k).wait_send()
@@ -340,7 +358,7 @@
             first_moves(me, crossing, lambda c: c.wait_send())
 
             def rest(f, carry):
-                for list_of in (after_early, after_first, after_relay, after_late):
+                for list_of in (after_first, after_third, after_relay, ahead):
                     for who, kind, src, slot, blk, rp in list_of(f):
                         if who == me:
                             move(kind, f, src, slot, blk, rp).wait_send()
@@ -357,10 +375,11 @@
     first = (lane % 64) < 32
     ids = rows_of(ids_ref[...])
 
-    def own(k):
-        vals = jnp.where(first, x_ref[0, k, 0:64, :], x_ref[1, k, 0:64, :])
-        theirs = jnp.where(first[0:8], x_ref[0, k, 64:72, :], x_ref[1, k, 64:72, :])
-        return vals, jnp.concatenate([theirs] * 8, axis=0)
+    def own(acc, v, upper):
+        turned = [pltpu.roll(x_ref[c, acc], (upper * 64 + (c - v) * HALF) % 128, 1) for c in range(2)]
+        both = jnp.where(first, turned[0][0:64, :], turned[1][0:64, :])
+        theirs = jnp.where(first[0:8], turned[0][64:72, :], turned[1][64:72, :])
+        return both, jnp.concatenate([theirs] * 8, axis=0)
 
     def taken(k, upper):
         both = jnp.concatenate([t_ref[0, k], t_ref[1, k]], axis=0)
@@ -380,11 +399,13 @@
                         parts.append(parts[0])
                         continue
                     if d == 0:
-                        vals, theirs = own(0)
+                        vals, theirs = own(0, 0, upper)
                         same = (theirs == ids) & ((lane % 64) != row)
                     else:
                         if d in OFFSETS[mine]:
-                            vals, theirs = own(1 + OFFSETS[mine].index(d))
+                            k = 1 + OFFSETS[mine].index(d)
+                            spot = (0, 1) if k == (3 if mine == 3 else 5) else (1, 2 if k in (3, 5) else (None, 0, 1, None, 3)[k])
+                            vals, theirs = own(*spot, upper)
                         else:
                             vals, theirs = taken(taken_at.index(d), upper)
                         same = theirs == ids
@@ -406,32 +427,32 @@
         main_kernel,
         in_specs=[in_vmem, in_vmem, pl.BlockSpec(memory_space=pl.ANY)],
         out_specs=[in_vmem] * 2,
-        out_shape=[jax.ShapeDtypeStruct((2, 6, 72, 128), f32), jax.ShapeDtypeStruct((2, 5, HALF, 128), f32)],
+        out_shape=[jax.ShapeDtypeStruct((2, 2, 72, 128), f32), jax.ShapeDtypeStruct((2, 5, HALF, 128), f32)],
         scratch_shapes=[
             vmem((4, GROUP, TOK, D), jnp.bfloat16),
             vmem((256, 256), jnp.bfloat16),
-            vmem((2, PIECES, 4, 2, GROUP, D), jnp.bfloat16),
+            vmem((2, PIECES, 2, 2, GROUP, D), jnp.bfloat16),
             vmem((64, 128), f32),
             vmem((64, 128), f32),
             vmem((2, 8, 128), f32),
-            vmem((7, PIECES, 4, 2, GROUP, D), jnp.bfloat16),
+            vmem((7, PIECES, 2, 2, GROUP, D), jnp.bfloat16),
             vmem((6, 8, 128), f32),
-            vmem((6, 2, ROWS, 128), f32),
-            vmem((6, 2, CHUNKS, HALF, CHUNK), f32),
-            vmem((6, 72, 128), f32),
-            vmem((6, 72, 128), f32),
-            vmem((6, HALF, 128), f32),
-            vmem((2, 6, HALF, 128), f32),
+            vmem((2, 2, ROWS, 128), f32),
+            vmem((2, 2, PIECES, HALF, 256), f32),
+            vmem((2, 72, 128), f32),
+            vmem((2, 72, 128), f32),
+            vmem((2, 128, 128), f32),
+            vmem((2, 5, HALF, 128), f32),
             dma((4,)),
             dma((8, PIECES)),
             dma((6, PIECES)),
             dma,
             dma((5,)),
             dma((5,)),
-            dma((6,)),
-            dma((6,)),
-            dma((2, 6)),
-            dma((2, 6)),
+            dma((2,)),
+            dma((2,)),
+            dma((2, 5)),
+            dma((2, 5)),
         ],
         compiler_params=pltpu.CompilerParams(collective_id=0, has_side_effects=True, vmem_limit_bytes=56 << 20),
     )(lens, ids, embeddings)

time: 90.7 us -> 102 us (1.12)
  Pallas kernels: 89.9 us -> 101 us
    pallas_call x1, Pallas kernels: 87.8 us -> 99.2 us  [shards(): pl.pallas_call(main_kernel, in_specs=[in_vmem, in_vmem, pl.BlockSpec(memo...]
where the time goes in v4:
time: 102 us
  Pallas kernels  101 us (99%)
    pallas_call x1, Pallas kernels, shards(): pl.pallas_call(main_kernel, in_specs=[in_vmem, in_vmem, pl.BlockSpec(memo...  99.2 us
    pallas_call x1, Pallas kernels, shards(): pl.pallas_call(place_kernel, in_specs=[pl.BlockSpec(memory_space=pltpu.SM...  2.09 us

profile of v4, /device:TPU:0, one launch (start us, length us, event | category | flops | bytes accessed | tf_op | source)
XLA Modules:
  0.0 102.0 jit_solution(16222075735219160335)
XLA Ops:
  0.6 99.2 %shard_map.50 = (f32[2,2,72,128]{3,2,1,0:T(8,128)}, f32[2,5,32,128]{3,2,1,0:T(8,128)}) custom-call(s32[1,64]{1,0:T(1,128)} %bitcast.6, s32[1,64]{1,0:T(1,128)} %bitcast.4, bf16[64,32,1024]{2,1,0:T(8,128)(2,1)} %emb_ref.1), custom_call_target="tpu_custom_call" | custom-call | tf_op jit(solution)/shard_map/pallas_call | solution.py:426
  99.9 2.1 %shard_map.51 = (f32[64,704]{1,0:T(8,128)}, f32[1,64]{1,0:T(1,128)}) custom-call(s32[1]{0:T(128)} %bitcast.role_ref, s32[1,64]{1,0:T(1,128)} %bitcast.5, f32[2,2,72,128]{3,2,1,0:T(8,128)} %get-tuple-element.6.x_ref, f32[2,5,32,128]{3,2,1,0:T(8,128)} %get-tuple-element.7.t_ref), custom_call_target="tpu_custom_call" | custom-call | tf_op jit(solution)/shard_map/pallas_call | solution.py:460
